TPU v7x, 32 devices: a whole 2x2x4 slice. The times are simulated.
32 devices in a mesh: blk: 4 (over y, x), py: 4 (over z), pz: 2 (over core).
Axes of the slice: x: 2, y: 2, z: 4, core: 2. Of those that a mesh axis runs over, the one named last changes fastest.
Arguments:
- source: float32 [256, 1024, 128], P(('py', 'pz'), 'blk'), may hold values from -6 to 6
- conduct: float32 [3], replicated, may hold values from 0.3 to 3
- neighbours: int32 [4, 2], replicated, may hold values from -1 to 3, as said below
- orient: int32 [4], replicated, may hold values 0 or 1
Outputs:
- solution: float32 [256, 1024, 128], P(('py', 'pz'), 'blk')
- norms: float32 [3], replicated
Inputs may be any that keep to these rules, and one draw needn't show every extreme that they name: `neighbours`: the blocks form one chain: row b holds the left and the right neighbour of block b, -1 marks the two ends, and a block is the left neighbour of its right neighbour.
All inputs are finite; a program needn't handle non-finite values.
Results may differ from a plain program's by a relative error of at most 0.00011.
Values sent between devices are 32-bit elements; how exact they have to be, the bound alone decides.
A program may use at most 128 MiB of HBM per device.

v0:
```python
import jax
import jax.numpy as jnp
from jax import lax
from jax.sharding import PartitionSpec as P

NY = 256
NZ = 128
BX = 256
OV = 64
ITERS = 3
EXT = 384


HIGHEST = lax.Precision.HIGHEST


def extended_2(cells, sides, width):
    for axis, dim in sides:
        count = lax.axis_size(axis)
        ends = count - 1
        head = lax.slice_in_dim(cells, 0, width, axis=dim)
        tail = lax.slice_in_dim(cells, cells.shape[dim] - width, cells.shape[dim], axis=dim)
        cells = jnp.concatenate(
            [
                lax.ppermute(tail, axis, [(i, (i + 1) % count) for i in range(ends)]),
                cells,
                lax.ppermute(head, axis, [((i + 1) % count, i) for i in range(ends)]),
            ],
            axis=dim,
        )
    return cells


def sine_basis(row_index, col_index, length):
    product = (row_index[:, None] + 1) * (col_index[None, :] + 1) % (2 * (length + 1))
    angles = jnp.pi * product.astype(jnp.float32) / (length + 1)
    return jnp.sqrt(2.0 / (length + 1)) * jnp.sin(angles)


def spectrum(index, length):
    angles = jnp.pi * (index.astype(jnp.float32) + 1.0) / (2.0 * (length + 1))
    return 4.0 * jnp.sin(angles) ** 2


def pick_block(pool, block_ids, wanted):
    match = (block_ids == wanted)[:, None, None, None]
    return jnp.sum(jnp.where(match, pool, 0.0), axis=0)


def outgoing(low_end, high_end, neighbours, own_block):
    left_of = (neighbours[:, 0] == own_block)[:, None, None, None]
    right_of = (neighbours[:, 1] == own_block)[:, None, None, None]
    return jnp.where(left_of, high_end[None], jnp.where(right_of, low_end[None], 0.0))


def shards(source, conduct, neighbours, orient):
    blocks = neighbours.shape[0]
    own_block = lax.axis_index("blk")
    block_ids = jnp.arange(blocks, dtype=jnp.int32)
    chosen = block_ids == own_block
    left_id = jnp.sum(jnp.where(chosen, neighbours[:, 0], 0))
    right_id = jnp.sum(jnp.where(chosen, neighbours[:, 1], 0))
    flipped = jnp.sum(jnp.where(chosen, orient, 0)) == 1
    has_left = (left_id >= 0).astype(jnp.float32)
    has_right = (right_id >= 0).astype(jnp.float32)
    planes_src = jnp.where(flipped, source[:, ::-1, :], source)
    size_py = lax.axis_size("py")
    size_pz = lax.axis_size("pz")
    group_size = size_py * size_pz
    group_width = EXT // group_size
    column_group = lax.axis_index("py") * size_pz + lax.axis_index("pz")
    plane_ids = jnp.arange(EXT, dtype=jnp.int32)
    row_ids = jnp.arange(NY, dtype=jnp.int32)
    depth_ids = jnp.arange(NZ, dtype=jnp.int32)
    plane_basis = sine_basis(plane_ids, plane_ids, EXT)
    row_basis = sine_basis(row_ids, row_ids, NY)
    depth_basis = sine_basis(depth_ids, depth_ids, NZ)
    held_modes = column_group * group_width + jnp.arange(group_width, dtype=jnp.int32)
    spectra = (
        conduct[0] * spectrum(held_modes, EXT)[None, :, None]
        + conduct[1] * spectrum(row_ids, NY)[:, None, None]
        + conduct[2] * spectrum(depth_ids, NZ)[None, None, :]
    )
    received = lax.all_to_all(
        outgoing(planes_src[:, :OV, :], planes_src[:, BX - OV :, :], neighbours, own_block),
        "blk",
        split_axis=0,
        concat_axis=0,
        tiled=True,
    )
    from_left = pick_block(received, block_ids, left_id)
    from_right = pick_block(received, block_ids, right_id)
    source_ext = jnp.concatenate([from_left, planes_src, from_right], axis=1)
    plane_mask = jnp.where(
        plane_ids < OV, has_left, jnp.where(plane_ids >= OV + BX, has_right, 1.0)
    )[None, :, None]
    cell_count = float(blocks * BX * NY * NZ)
    iterate = jnp.zeros_like(planes_src)
    square_sums = []
    for iteration in range(ITERS):
        if iteration == 0:
            residual = source_ext * plane_mask
        else:
            iterate_received = lax.all_to_all(
                outgoing(
                    iterate[:, : OV + 1, :], iterate[:, BX - OV - 1 :, :], neighbours, own_block
                ),
                "blk",
                split_axis=0,
                concat_axis=0,
                tiled=True,
            )
            iterate_left = pick_block(iterate_received, block_ids, left_id)
            iterate_right = pick_block(iterate_received, block_ids, right_id)
            extended = jnp.concatenate([iterate_left, iterate, iterate_right], axis=1)
            centre = extended[:, 1:-1, :]
            rows_pad = extended_2(centre, ((("py", "pz"), 0),), 1)
            depth_pad = jnp.pad(centre, ((0, 0), (0, 0), (1, 1)))
            applied = (
                conduct[0] * (2.0 * centre - extended[:, :-2, :] - extended[:, 2:, :])
                + conduct[1] * (2.0 * centre - rows_pad[:-2] - rows_pad[2:])
                + conduct[2] * (2.0 * centre - depth_pad[:, :, :-2] - depth_pad[:, :, 2:])
            )
            residual = (source_ext - applied) * plane_mask
        own_squares = jnp.sum(residual[:, OV : OV + BX, :] ** 2)
        square_sums.append(lax.psum(own_squares, ("blk", "py", "pz")))
        modes = jnp.einsum("yxz,xk->ykz", residual, plane_basis, precision=HIGHEST)
        columns = lax.all_to_all(modes, ("py", "pz"), split_axis=1, concat_axis=0, tiled=True)
        columns = jnp.einsum("lxz,lm->mxz", columns, row_basis, precision=HIGHEST)
        columns = jnp.einsum("yxz,zk->yxk", columns, depth_basis, precision=HIGHEST)
        columns = columns / spectra
        columns = jnp.einsum("yxz,zk->yxk", columns, depth_basis, precision=HIGHEST)
        columns = jnp.einsum("mxz,ym->yxz", columns, row_basis, precision=HIGHEST)
        returned = lax.all_to_all(columns, ("py", "pz"), split_axis=0, concat_axis=1, tiled=True)
        iterate = (
            iterate
            + jnp.einsum("ypz,xp->yxz", returned, plane_basis, precision=HIGHEST)[
                :, OV : OV + BX, :
            ]
        )
    norms = jnp.sqrt(jnp.stack(square_sums) / cell_count)
    solution = jnp.where(flipped, iterate[:, ::-1, :], iterate)
    return (solution, norms)


def solution(mesh):
    placed = (P(("py", "pz"), "blk", None), P(), P(), P())
    return jax.shard_map(
        shards,
        mesh=mesh,
        in_specs=placed,
        out_specs=(P(("py", "pz"), "blk", None), P()),
        check_vma=False,
    )
```

profile of v0, /device:TPU:0, one launch (start us, length us, event | category | flops | bytes accessed | tf_op | source)
XLA Modules:
  0.0 1430.0 jit_solution(5636458374781292929)
XLA Ops:
  0.6 1.3 select_reduce_fusion.6
  2.7 32.5 %rev.6 = f32[32,256,128]{2,1,0:T(8,128)} reverse(f32[32,256,128]{2,1,0:T(8,128)} %param.4), dimensions={1} | reverse | bytes 8388608 | tf_op jit(solution)/shard_map/rev | solution.py:66
  35.8 2.7 broadcast_select_fusion.1
  38.5 2.0 copy-done.2
  40.7 2.6 select_select_fusion.2
  43.3 5.2 all-to-all-start
  51.6 45.5 %all-to-all-done = f32[4,32,64,128]{3,2,1,0:T(8,128)} async-done(((f32[4,32,64,128]{3,2,1,0:T(8,128)}), f32[4,32,64,128]{3,2,1,0:T(8,128)}, u32[]{:S(2)}, u32[]{:S(2)}) %all-to-all-start) | async-done | bytes 4194336 | tf_op jit(solution)/shard_map/all_to_all | solution.py:84
  97.1 3.3 select_reduce_fusion.5
  103.0 2.7 copy-done.6
  105.6 25.6 %convolution_bitcast_fusion.5 = f32[32,384,128]{2,1,0:T(8,128)S(1)} fusion(f32[32,384,128]{2,1,0:T(8,128)S(1)} %broadcast_multiply_fusion, s32[384]{0:T(512)S(1)} %iota_add_fusion), kind=kOutput, calls=%fused_computation.81 | convolution fusion | flops 7249231872 | bytes 12584448 | tf_op jit(solution)/shard_map/yxz,xk->ykz/dot_general | solution.py:127
  131.2 6.2 copy.122
  137.5 5.2 all-to-all-start.1
  145.4 136.2 %all-to-all-done.1 = f32[32,384,128]{2,0,1:T(8,128)} async-done(((f32[32,384,128]{2,0,1:T(8,128)}), f32[32,384,128]{2,0,1:T(8,128)}, u32[]{:S(2)}, u32[]{:S(2)}) %all-to-all-start.1) | async-done | bytes 6291488 | tf_op jit(solution)/shard_map/all_to_all | solution.py:128
  281.7 6.3 copy.124
  288.0 9.1 fusion.40
  297.2 9.6 add_divide_fusion.2
  306.8 7.6 fusion.36
  314.4 7.8 fusion.116
  322.2 3.6 copy.129
  325.9 141.4 %all_to_all.123 = f32[256,48,128]{2,1,0:T(8,128)S(1)} all-to-all(f32[256,48,128]{2,1,0:T(8,128)S(1)} %copy.129), channel_id=1, replica_groups=mesh['blk'=4,'py'=4,'pz'=2] {'py','pz'}, dimensions={0} | all-to-all | bytes 12582912 | tf_op jit(solution)/shard_map/all_to_all | solution.py:134
  468.1 12.4 convolution_bitcast_fusion.4
  480.6 2.6 copy-done.5
  484.0 2.7 select_select_fusion.1
  486.7 4.9 all-to-all-start.3
  491.6 4.7 slice.164
  496.3 43.4 %all-to-all-done.3 = f32[4,32,65,128]{3,1,2,0:T(8,128)} async-done(((f32[4,32,65,128]{3,1,2,0:T(8,128)}), f32[4,32,65,128]{3,1,2,0:T(8,128)}, u32[]{:S(2)}, u32[]{:S(2)}) %all-to-all-start.3) | async-done | bytes 4259872 | tf_op jit(solution)/shard_map/all_to_all | solution.py:104
  539.6 3.4 select_reduce_fusion.3
  544.3 1.3 collective-permute-start
  549.6 10.1 fusion.5
  559.7 13.8 convolution_bitcast_fusion.3
  573.6 3.6 copy.136
  577.2 145.7 %all_to_all.124 = f32[32,384,128]{2,0,1:T(8,128)S(1)} all-to-all(f32[32,384,128]{2,0,1:T(8,128)S(1)} %copy.136), channel_id=1, replica_groups=mesh['blk'=4,'py'=4,'pz'=2] {'py','pz'}, dimensions={1} | all-to-all | bytes 12582912 | tf_op jit(solution)/shard_map/all_to_all | solution.py:128
  723.0 3.6 copy.138
  726.5 9.1 fusion.34
  735.7 9.6 add_divide_fusion.1
  745.3 7.8 fusion.30
  753.1 7.6 fusion.114
  760.7 3.6 copy.143
  764.4 141.4 %all_to_all.125 = f32[256,48,128]{2,1,0:T(8,128)S(1)} all-to-all(f32[256,48,128]{2,1,0:T(8,128)S(1)} %copy.143), channel_id=1, replica_groups=mesh['blk'=4,'py'=4,'pz'=2] {'py','pz'}, dimensions={0} | all-to-all | bytes 12582912 | tf_op jit(solution)/shard_map/all_to_all | solution.py:134
  906.6 12.8 convolution_bitcast_fusion.2
  921.8 51.2 %all_to_all.126 = f32[4,32,65,128]{3,1,2,0:T(8,128)S(1)} all-to-all(f32[4,32,65,128]{3,1,2,0:T(8,128)S(1)} %select_select_fusion), channel_id=1, replica_groups=mesh['blk'=4,'py'=4,'pz'=2] {'blk'}, dimensions={0} | all-to-all | bytes 8519680 | tf_op jit(solution)/shard_map/all_to_all | solution.py:104
  977.0 1.3 collective-permute-start.3
  978.8 3.4 slice.173
  982.2 18.5 %fusion.11 = f32[32,384,128]{2,1,0:T(8,128)S(1)} fusion(f32[32,384,128]{2,1,0:T(8,128)} %slice.173, f32[1,384,128]{2,1,0:T(8,128)S(1)} %collective-permute-done.3, f32[1,384,128]{2,1,0:T(8,128)S(1)} %collective-permute-done.2, f32[32,386,128]{2,1,0:T(8,128)S(1)} %pad_maximum_fusion.1, f32[]{:T(128)} %bitcast.14, f32[]{:T(128)} %bitcast.13, f32[]{:T(128)} %bitcast.12, ...), kind=kLoop, calls=%fused_computation.20 | loop fusion | flops 28311552 | bytes 31852044 | tf_op jit(solution)/shard_map/mul | solution.py:124
  1000.7 13.6 convolution_bitcast_fusion.1
  1014.4 3.6 copy.150
  1018.0 144.8 %all_to_all.127 = f32[32,384,128]{2,0,1:T(8,128)S(1)} all-to-all(f32[32,384,128]{2,0,1:T(8,128)S(1)} %copy.150), channel_id=1, replica_groups=mesh['blk'=4,'py'=4,'pz'=2] {'py','pz'}, dimensions={1} | all-to-all | bytes 12582912 | tf_op jit(solution)/shard_map/all_to_all | solution.py:128
  1162.9 3.6 copy.152
  1166.4 9.4 fusion.28
  1175.8 9.6 add_divide_fusion
  1185.4 8.5 fusion.24
  1194.0 7.6 fusion.112
  1201.6 6.2 copy.157
  1207.8 4.8 all-to-all-start.8
  1212.6 3.9 fusion.44
  1216.6 3.9 fusion.43
  1220.5 3.9 fusion.42
  1224.4 146.6 %all-reduce.2 = (f32[1]{0:T(128)}, f32[1]{0:T(128)}, f32[1]{0:T(128)}) all-reduce(f32[1]{0:T(128)} %bitcast.43, f32[1]{0:T(128)} %bitcast.42, f32[1]{0:T(128)} %bitcast.41), channel_id=1, replica_groups=mesh['blk'=4,'py'=4,'pz'=2] {'blk','py','pz'}, use_global_device_ids=true, to_apply=%region_14.15 | all-reduce | flops 3 | bytes 24 | tf_op jit(solution)/shard_map/psum | solution.py:126
  1371.0 2.6 fusion.204
  1373.6 3.6 copy.158
  1377.2 12.8 convolution_bitcast_fusion
  1390.1 2.5 slice_add_fusion
  1392.6 32.3 %rev.7 = f32[32,256,128]{2,1,0:T(8,128)} reverse(f32[32,256,128]{2,1,0:T(8,128)} %slice_add_fusion), dimensions={1} | reverse | bytes 8388608 | tf_op jit(solution)/shard_map/rev | solution.py:142
  1424.9 4.9 broadcast_select_fusion
  (81 shorter events, 20.5 us)
Async XLA Ops:
  38.5 2.0 copy-start.2
  40.7 7.8 copy-start.18
  43.3 53.8 %all-to-all-start = ((f32[4,32,64,128]{3,2,1,0:T(8,128)}), f32[4,32,64,128]{3,2,1,0:T(8,128)}, u32[]{:S(2)}, u32[]{:S(2)}) async-start(f32[4,32,64,128]{3,2,1,0:T(8,128)} %select_select_fusion.2), calls=%async_computation | async-start | bytes 8388608 | tf_op jit(solution)/shard_map/all_to_all | solution.py:84
  97.1 4.7 copy-start.3
  100.5 1.0 copy-start.10
  100.5 1.3 copy-start.12
  102.9 2.7 copy-start.6
  137.4 5.2 copy-start.17
  137.5 144.2 %all-to-all-start.1 = ((f32[32,384,128]{2,0,1:T(8,128)}), f32[32,384,128]{2,0,1:T(8,128)}, u32[]{:S(2)}, u32[]{:S(2)}) async-start(f32[32,384,128]{2,0,1:T(8,128)} %copy.122), calls=%async_computation.1 | async-start | bytes 12582912 | tf_op jit(solution)/shard_map/all_to_all | solution.py:128
  145.4 151.7 %copy-start.14 = (f32[256,48]{1,0:T(8,128)}, f32[256,48]{1,0:T(8,128)S(1)}, u32[]{:S(2)}) copy-start(f32[256,48]{1,0:T(8,128)S(1)} %broadcast_add_fusion) | copy-start | bytes 147460
  480.6 2.6 copy-start.5
  486.7 52.9 %all-to-all-start.3 = ((f32[4,32,65,128]{3,1,2,0:T(8,128)}), f32[4,32,65,128]{3,1,2,0:T(8,128)}, u32[]{:S(2)}, u32[]{:S(2)}) async-start(f32[4,32,65,128]{3,1,2,0:T(8,128)} %select_select_fusion.1), calls=%async_computation.3 | async-start | bytes 8519680 | tf_op jit(solution)/shard_map/all_to_all | solution.py:104
  539.6 4.7 copy-start.9
  544.3 3.9 collective-permute-start
  545.6 3.3 collective-permute-start.1
  547.4 2.2 copy-start.4
  559.7 13.9 copy-start.7
  726.5 9.1 copy-start.15
  905.8 13.6 slice-start
  906.5 12.9 slice-start.1
  920.5 57.8 %copy-start = (f32[32,256,128]{2,1,0:T(8,128)}, f32[32,256,128]{2,1,0:T(8,128)S(1)}, u32[]{:S(2)}) copy-start(f32[32,256,128]{2,1,0:T(8,128)S(1)} %slice_add_fusion.1) | copy-start | bytes 12582916
  975.7 6.5 collective-permute-start.2
  977.0 5.2 collective-permute-start.3
  978.8 3.4 copy-start.11
  978.8 3.4 copy-start.13
  1000.7 13.6 copy-start.8
  1166.4 9.4 copy-start.16
  1207.8 165.8 %all-to-all-start.8 = ((f32[256,48,128]{2,1,0:T(8,128)}), f32[256,48,128]{2,1,0:T(8,128)}, u32[]{:S(2)}, u32[]{:S(2)}) async-start(f32[256,48,128]{2,1,0:T(8,128)} %copy.157), calls=%async_computation.8 | async-start | bytes 12582912 | tf_op jit(solution)/shard_map/all_to_all | solution.py:134
  1377.2 12.9 copy-start.1
where the time goes:
time: 1430 us
  blocking collectives  771 us (54%)
  waiting for transfers between devices  226 us (16%)
  matrix products  195 us (14%)
  local copies, waits for them, and re-layouts  133 us (9%)
  other arithmetic  74.4 us (5%)
  starting transfers between devices  25.2 us (2%)
    all_to_all x2, blocking collectives, shards(): lax.all_to_all(modes, ('py', 'pz'), split_axis=1, concat_axis=0, tiled=True)  291 us
    all_to_all x2, blocking collectives, shards(): lax.all_to_all(columns, ('py', 'pz'), split_axis=0, concat_axis=1, tiled=...  283 us
    psum x1, blocking collectives, shards(): square_sums.append(lax.psum(own_squares, ('blk', 'py', 'pz')))  147 us
    all_to_all x1, waiting for transfers between devices, shards(): lax.all_to_all(modes, ('py', 'pz'), split_axis=1, concat_axis=0, tiled=True)  136 us
    dot_general x3, matrix products, shards(): modes = jnp.einsum('yxz,xk->ykz', residual, plane_basis, precision=HIGHEST)  53 us
    dot_general x6, matrix products, shards(): columns = jnp.einsum('yxz,zk->yxk', columns, depth_basis, precision=HIGHEST)  52.8 us
    all_to_all x1, blocking collectives, shards(): lax.all_to_all(outgoing(iterate[:, :OV + 1, :], iterate[:, BX - OV - 1:,...  51.2 us
    all_to_all x1, waiting for transfers between devices, shards(): lax.all_to_all(outgoing(planes_src[:, :OV, :], planes_src[:, BX - OV:, :]...  45.5 us
  transfers between devices with their start and end apart: 8, of which 4 were waited for; matrix products, arithmetic and copies ran while one was open for 2% of the time, Pallas kernels for 0%

commit v1 on v0

v1 whole, which is shorter than its diff:
```python
import jax
import jax.numpy as jnp
import numpy as np
from jax import lax
from jax.sharding import PartitionSpec as P

OV = 64
ITERS = 3

HIGHEST = lax.Precision.HIGHEST
HIGH = lax.Precision.HIGH


def sine_basis(row_index, col_index, length):
    product = (row_index[:, None] + 1) * (col_index[None, :] + 1) % (2 * (length + 1))
    values = np.sqrt(2.0 / (length + 1)) * np.sin(np.pi * product / (length + 1))
    return values.astype(np.float32)


def spectrum(length):
    angles = np.pi * (np.arange(length) + 1.0) / (2.0 * (length + 1))
    return (4.0 * np.sin(angles) ** 2).astype(np.float32)


def plane_tables(planes):
    ids = np.arange(planes)
    small = np.arange(OV - 1)
    own = sine_basis(ids, ids, planes)
    margin = sine_basis(small, small, OV - 1)
    count = planes + 2 * (OV - 1) + 2
    at_tail = planes
    at_head = planes + OV - 1
    forward = np.zeros((planes, count), np.float32)
    forward[:, :planes] = own
    forward[planes - OV : planes - 1, at_tail:at_head] = margin
    forward[1:OV, at_head : at_head + OV - 1] = margin
    forward[planes - 1, count - 2] = 1.0
    forward[0, count - 1] = 1.0
    mu = np.ones((count,), np.float32)
    mu[:planes] = spectrum(planes)
    mu[at_tail:at_head] = spectrum(OV - 1)
    mu[at_head : at_head + OV - 1] = spectrum(OV - 1)
    box_pick = np.zeros((count, 4), np.float32)
    box_pick[:planes, 0] = own[0]
    box_pick[:planes, 1] = own[-1]
    margin_pick = np.zeros((count, 4), np.float32)
    margin_pick[at_tail:at_head, 2] = margin[-1]
    margin_pick[at_head : at_head + OV - 1, 3] = margin[0]
    return own, forward, mu, box_pick, margin_pick


def shift_blocks(values, ids):
    blocks = ids.shape[0]
    match = (ids[:, None] == jnp.arange(blocks, dtype=jnp.int32)[None, :]).astype(jnp.float32)
    rows = []
    for b in range(blocks):
        total = match[b, 0] * values[0]
        for other in range(1, blocks):
            total = total + match[b, other] * values[other]
        rows.append(total)
    return jnp.stack(rows)


def shards(source, conduct, neighbours, orient):
    blocks = neighbours.shape[0]
    rows, planes, depth = source.shape
    group = lax.axis_size("py") * lax.axis_size("pz")
    all_rows = rows * group
    own_depth = depth // group
    own_block = lax.axis_index("blk")
    member = lax.axis_index("py") * lax.axis_size("pz") + lax.axis_index("pz")
    chosen = jnp.arange(blocks, dtype=jnp.int32) == own_block
    flipped = jnp.sum(jnp.where(chosen, orient, 0)) == 1
    c0, c1, c2 = conduct[0], conduct[1], conduct[2]

    own, forward, mu_plane, box_pick, margin_pick = plane_tables(planes)
    count = forward.shape[1]
    row_ids = np.arange(all_rows)
    local_ids = np.arange(rows)
    depth_ids = np.arange(depth)
    row_basis = jnp.asarray(sine_basis(row_ids, row_ids, all_rows))
    local_basis = jnp.asarray(sine_basis(local_ids, local_ids, rows))
    depth_basis = jnp.asarray(sine_basis(depth_ids, depth_ids, depth))
    beside = np.stack([rows * np.arange(group) - 1, rows * (np.arange(group) + 1)], axis=1)
    beside_basis = sine_basis(beside.reshape(-1), row_ids, all_rows)
    beside_basis = beside_basis.reshape(group, 2, all_rows)
    beside_basis[0, 0] = 0.0
    beside_basis[-1, 1] = 0.0
    beside_basis = jnp.asarray(beside_basis)
    mu_row = jnp.asarray(spectrum(all_rows))
    mu_local = jnp.asarray(spectrum(rows))
    mu_depth = jnp.asarray(spectrum(depth))
    mu_plane = jnp.asarray(mu_plane)
    own_table = jnp.asarray(own)
    first_col, last_col = own_table[0], own_table[-1]
    forward = jnp.asarray(forward)
    forward = jnp.where(flipped, forward[::-1], forward)
    backward = jnp.where(flipped, own_table[::-1], own_table)
    pick = jnp.asarray(box_pick) + c0 * jnp.asarray(margin_pick)

    cells = jnp.einsum("ypz,zk->ypk", source, depth_basis, precision=HIGH)
    cells = jnp.einsum("ypk,pi->yik", cells, forward, precision=HIGH)
    modes = jnp.einsum("yik,ym->mik", cells, local_basis, precision=HIGH)
    slab_spectra = (
        c0 * mu_plane[None, :, None]
        + c1 * mu_local[:, None, None]
        + c2 * mu_depth[None, None, :]
    )
    slab = modes / slab_spectra
    edges = jnp.einsum("mik,em->eki", slab, local_basis[jnp.array([0, rows - 1])], precision=HIGH)
    ends = jnp.einsum("mik,iq->mqk", slab, pick, precision=HIGH)
    ends = jnp.einsum("mqk,ym->kqy", ends, local_basis, precision=HIGH)
    plain = jnp.zeros((2, rows, depth), jnp.float32)
    plain = jnp.concatenate([plain, jnp.stack([cells[:, count - 2], cells[:, count - 1]])], axis=0)
    ends = ends + jnp.transpose(plain, (2, 0, 1))

    packed = jnp.concatenate([edges[0], edges[1], ends.reshape(depth, 4 * rows)], axis=1)
    packed = lax.all_to_all(packed, ("py", "pz"), split_axis=0, concat_axis=0, tiled=True)
    packed = packed.reshape(group, own_depth, 2 * count + 4 * rows)
    edge_first = packed[:, :, :count]
    edge_last = packed[:, :, count : 2 * count]
    ends = packed[:, :, 2 * count :].reshape(group, own_depth, 4, rows)

    empty = jnp.zeros_like(edge_first[:1])
    below = jnp.concatenate([empty, edge_last[:-1]], axis=0)
    above = jnp.concatenate([edge_first[1:], empty], axis=0)
    first_rows = row_basis[rows * np.arange(group)]
    last_rows = row_basis[rows * np.arange(group) + rows - 1]
    seam_basis = jnp.concatenate([first_rows, last_rows], axis=0)
    seams = jnp.concatenate([below, above], axis=0)
    joined = c1 * jnp.einsum("rki,rj->kji", seams, seam_basis, precision=HIGH)
    held_depth = lax.dynamic_slice_in_dim(mu_depth, member * own_depth, own_depth)
    cross = c1 * mu_row[None, :] + c2 * held_depth[:, None]
    spectra = c0 * mu_plane[None, None, :] + cross[:, :, None]
    moments = jnp.einsum("kji,iq->qkj", joined / spectra, pick, precision=HIGH)
    moments = moments + jnp.einsum(
        "dkqy,dyj->qkj", ends, row_basis.reshape(group, rows, all_rows), precision=HIGHEST
    )
    every = lax.all_gather(moments, "blk", axis=0)

    half = 0.5 * jnp.sqrt(cross / c0)
    root = jnp.sqrt(1.0 + half * half)
    theta = 2.0 * jnp.log1p(half + half * half / (1.0 + root))
    sinh = 2.0 * half * root

    def tanh_of(n):
        decay = jnp.exp(-2.0 * n * theta)
        return -jnp.expm1(-2.0 * n * theta) / (1.0 + decay)

    outer = 1.0 / tanh_of(float(OV))
    mid = tanh_of(0.5 * (planes + 1))
    even_inv = 1.0 / (sinh * (outer + mid))
    odd_inv = 1.0 / (sinh * (outer + 1.0 / mid))
    reach = jnp.exp(-(planes + 1.0) * theta)
    span = -jnp.expm1(-2.0 * (planes + 1.0) * theta)
    beta = sinh * 2.0 * reach / span
    alpha = jnp.exp(-theta) * -jnp.expm1(-2.0 * planes * theta) / span

    left_ids, right_ids = neighbours[:, 0], neighbours[:, 1]
    own_low, own_high = every[:, 0], every[:, 1]
    beyond_low = shift_blocks(every[:, 2], left_ids) / c0
    beyond_high = shift_blocks(every[:, 3], right_ids) / c0
    push_low = jnp.zeros_like(own_low)
    push_high = jnp.zeros_like(own_low)
    squares = [jnp.sum(source * source)]
    for iteration in range(ITERS):
        drive_low = beyond_low + own_low
        drive_high = beyond_high + own_high
        even = (drive_low + drive_high) * even_inv
        odd = (drive_low - drive_high) * odd_inv
        low = 0.5 * (even + odd)
        high = 0.5 * (even - odd)
        push_low = push_low + low
        push_high = push_high + high
        if iteration == ITERS - 1:
            break
        inner_low = own_low + alpha * low + beta * high
        inner_high = own_high + beta * low + alpha * high
        jump_low = shift_blocks(inner_high, left_ids) - low
        jump_high = shift_blocks(inner_low, right_ids) - high
        held = jnp.where(chosen[:, None, None], jump_low**2 + jump_high**2, 0.0)
        squares.append(c0 * c0 * jnp.sum(held))
        push_low = push_low + jump_low
        push_high = push_high + jump_high
        own_low = alpha * jump_low + beta * jump_high
        own_high = beta * jump_low + alpha * jump_high
        beyond_low = shift_blocks(jump_high, left_ids)
        beyond_high = shift_blocks(jump_low, right_ids)
    pushes = c0 * jnp.stack([push_low, push_high], axis=1)
    pushes = jnp.sum(jnp.where(chosen[:, None, None, None], pushes, 0.0), axis=0)

    total = (
        joined[:, :, :planes]
        + pushes[0][:, :, None] * first_col
        + pushes[1][:, :, None] * last_col
    )
    total = total / spectra[:, :, :planes]
    beside_values = jnp.einsum("kji,dsj->dksi", total, beside_basis, precision=HIGH)
    beside_values = beside_values + jnp.stack([below, above], axis=2)[:, :, :, :planes]
    pushes = jnp.einsum(
        "skj,dyj->dksy", pushes, row_basis.reshape(group, rows, all_rows), precision=HIGHEST
    )
    packed = jnp.concatenate(
        [
            beside_values.reshape(group, own_depth, 2 * planes),
            pushes.reshape(group, own_depth, 2 * rows),
        ],
        axis=2,
    ).reshape(depth, 2 * planes + 2 * rows)
    packed = lax.all_to_all(packed, ("py", "pz"), split_axis=0, concat_axis=0, tiled=True)
    packed = jnp.transpose(packed)
    below = packed[:planes]
    above = packed[planes : 2 * planes]
    pushes = jnp.einsum(
        "syk,ym->smk",
        packed[2 * planes :].reshape(2, rows, depth),
        local_basis,
        precision=HIGHEST,
    )

    modes = (
        modes[:, :planes]
        + c1 * local_basis[0][:, None, None] * below
        + c1 * local_basis[-1][:, None, None] * above
        + first_col[None, :, None] * pushes[0][:, None, :]
        + last_col[None, :, None] * pushes[1][:, None, :]
    ) / slab_spectra[:, :planes]
    cells = jnp.einsum("mik,ym->yik", modes, local_basis, precision=HIGH)
    cells = jnp.einsum("yik,pi->ypk", cells, backward, precision=HIGH)
    solution = jnp.einsum("ypk,zk->ypz", cells, depth_basis, precision=HIGH)

    cell_count = float(blocks * planes * all_rows * depth)
    sums = lax.psum(jnp.stack(squares), ("blk", "py", "pz"))
    return (solution, jnp.sqrt(sums / cell_count))


def solution(mesh):
    placed = (P(("py", "pz"), "blk", None), P(), P(), P())
    return jax.shard_map(
        shards,
        mesh=mesh,
        in_specs=placed,
        out_specs=(P(("py", "pz"), "blk", None), P()),
        check_vma=False,
    )
```

time: 1430 us -> 259 us (0.18)
  blocking collectives: 771 us -> 49.1 us
  waiting for transfers between devices: 226 us -> 1.52 us
  matrix products: 195 us -> 56.6 us
  local copies, waits for them, and re-layouts: 133 us -> 8.93 us
  other arithmetic: 74.4 us -> 126 us
  starting transfers between devices: 25.2 us -> 9.93 us
    all_to_all x5 -> x0, blocking collectives: 625 us -> none  [the longest x2 291 us: shards(): lax.all_to_all(modes, ('py', 'pz'), split_axis=1, concat_axis=0, tiled=True)]
    all_to_all x4 -> x2, waiting for transfers between devices: 225 us -> 1.52 us  [shards(): lax.all_to_all(packed, ('py', 'pz'), split_axis=0, concat_axis=0, tiled=T...]
    dot_general x18 -> x15, matrix products: 195 us -> 56.6 us  [the longest x1 11.7 us: shards(): modes = jnp.einsum('yik,ym->mik', cells, local_basis, precision=HIGH)]
    psum x1, blocking collectives: 147 us -> 40.1 us  [shards(): sums = lax.psum(jnp.stack(squares), ('blk', 'py', 'pz'))]
    add x6 -> x28, other arithmetic: 3.71 us -> 91.4 us  [the longest x19 86 us: shift_blocks(): total = total + match[b, other] * values[other]]
    rev x2 -> x0, local copies, waits for them, and re-layouts: 64.8 us -> none  [the longest x1 32.5 us: shards(): planes_src = jnp.where(flipped, source[:, ::-1, :], source)]
    mul x6 -> x7, other arithmetic: 29.9 us -> 4.58 us  [the longest x2 1.32 us: shards(): cross = c1 * mu_row[None, :] + c2 * held_depth[:, None]]
    another operation x0 -> x6, other arithmetic: none -> 20.9 us  [the longest x4 20.2 us: shift_blocks(): return jnp.stack(rows)]
  transfers between devices with their start and end apart: 8 -> 2, of which waited for: 4 -> 1; matrix products, arithmetic and copies ran while one was open for 2% -> 5% of each run, Pallas kernels for 0% -> 0%
where the time goes in v1:
time: 259 us; the launch traced here: 256 us
  other arithmetic  126 us (49%)
  matrix products  56.6 us (22%)
  blocking collectives  49.1 us (19%)
  starting transfers between devices  9.93 us (4%)
  local copies, waits for them, and re-layouts  8.93 us (3%)
  between operations  4.65 us (2%)
    add x19, other arithmetic, shift_blocks(): total = total + match[b, other] * values[other]  86 us
    psum x1, blocking collectives, shards(): sums = lax.psum(jnp.stack(squares), ('blk', 'py', 'pz'))  40.1 us
    another operation x4, other arithmetic, shift_blocks(): return jnp.stack(rows)  20.2 us
    dot_general x1, matrix products, shards(): modes = jnp.einsum('yik,ym->mik', cells, local_basis, precision=HIGH)  11.7 us
    all_to_all x2, starting transfers between devices, shards(): lax.all_to_all(packed, ('py', 'pz'), split_axis=0, concat_axis=0, tiled=T...  9.93 us
    all_gather x1, blocking collectives, shards(): every = lax.all_gather(moments, 'blk', axis=0)  8.99 us
    dot_general x1, matrix products, shards(): cells = jnp.einsum('mik,ym->yik', modes, local_basis, precision=HIGH)  6.31 us
    dot_general x1, matrix products, shards(): ends = jnp.einsum('mik,iq->mqk', slab, pick, precision=HIGH)  5.49 us
  transfers between devices with their start and end apart: 2, of which 1 were waited for; matrix products, arithmetic and copies ran while one was open for 5% of the time, Pallas kernels for 0%

profile of v1, /device:TPU:0, one launch (start us, length us, event | category | flops | bytes accessed | tf_op | source)
XLA Modules:
  0.0 256.4 jit_solution(16802336624897823851)
XLA Ops:
  0.6 1.4 fusion.110
  2.1 1.3 select_reduce_fusion.2
  4.0 4.2 %fusion.111 = f32[128,32,256]{2,0,1:T(8,128)S(1)} fusion(f32[128,128,1]{0,1,2:T(8,128)} %constant.116, f32[32,256,128]{2,1,0:T(8,128)} %param.21), kind=kOutput, calls=%fused_computation.237 | convolution fusion | flops 805306368 | bytes 8454144 | tf_op jit(solution)/shard_map/ypz,zk->ypk/dot_general | solution.py:101
  8.3 3.0 %fusion.28 = f32[32,384,128]{2,1,0:T(8,128)S(1)} fusion(f32[128,32,256]{2,0,1:T(8,128)S(1)} %fusion.111, f32[256,384]{0,1:T(8,128)S(1)} %copy-done.4, f32[256,384]{0,1:T(8,128)S(1)} %copy-done.5, pred[]{:T(512)S(6)} %eq.32), kind=kOutput, calls=%fused_computation.35 | convolution fusion | flops 2416017408 | bytes 11272193 | tf_op jit(solution)/shard_map/ypk,pi->yik/dot_general | solution.py:102
  11.4 0.7 broadcast_multiply_fusion.2
  12.1 0.6 broadcast_multiply_fusion.5
  12.8 0.7 broadcast_multiply_fusion.4
  13.5 11.7 %fusion.43 = (f32[32,384,128]{2,0,1:T(8,128)S(1)}, f32[32,384,128]{2,0,1:T(8,128)}, f32[32,384,128]{2,0,1:T(8,128)}) fusion(f32[128]{0:T(128)S(1)} %broadcast_multiply_fusion.4, f32[32,384]{0,1:T(8,128)S(1)} %broadcast_add_fusion.3, f32[32,32,1]{1,0,2:T(8,128)S(1)} %copy-done.8, f32[32,384,128]{2,1,0:T(8,128)S(1)} %fusion.28), kind=kOutput, calls=%fused_computation.48 | convolution fusion | flops 305135616 | bytes 25219584 | tf_op jit(solution)/shard_map/yik,ym->mik/dot_general | solution.py:103
  25.3 2.6 %copy-done = f32[32,384,128]{2,0,1:T(8,128)} copy-done((f32[32,384,128]{2,0,1:T(8,128)}, f32[32,384,128]{2,0,1:T(8,128)S(1)}, u32[]{:S(2)}) %copy-start) | copy-done | bytes 6291480
  27.9 5.5 %fusion.50 = f32[32,4,128]{2,1,0:T(4,128)S(1)} fusion(f32[32,384,128]{2,0,1:T(8,128)S(1)} %get-tuple-element.28, f32[384,4]{0,1:T(4,128)S(1)} %copy-done.10, f32[384,4]{0,1:T(4,128)S(1)} %copy-done.11, f32[]{:T(128)} %bitcast.10), kind=kOutput, calls=%fused_computation.53 | convolution fusion | flops 37751808 | bytes 6369284 | tf_op jit(solution)/shard_map/mik,iq->mqk/dot_general | solution.py:111
  33.9 0.6 gather_fusion.1
  34.5 4.5 %convolution_bitcast_fusion = f32[2,128,384]{1,0,2:T(2,128)S(1)} fusion(f32[32,384,128]{2,0,1:T(8,128)} %copy-done, f32[2,32]{1,0:T(2,128)S(1)} %gather_fusion.1), kind=kOutput, calls=%fused_computation.49 | convolution fusion | flops 18874368 | bytes 6684928 | tf_op jit(solution)/shard_map/mik,em->eki/dot_general | solution.py:110
  39.6 0.8 pad_maximum_fusion
  40.4 6.4 %all-to-all-start = ((f32[8,16,896]{2,1,0:T(8,128)}), f32[8,16,896]{2,1,0:T(8,128)S(1)}, u32[]{:S(2)}, u32[]{:S(2)}) async-start(f32[8,16,896]{2,1,0:T(8,128)} %pad_maximum_fusion), calls=%async_computation | async-start | bytes 917504 | tf_op jit(solution)/shard_map/all_to_all | solution.py:118
  46.8 0.7 dynamic-slice_multiply_fusion
  47.5 0.6 broadcast_multiply_fusion.3
  48.2 0.7 fusion.108
  48.9 0.8 broadcast_multiply_fusion.1
  51.0 0.6 gather_fusion
  51.6 0.7 fusion.109
  52.3 3.9 %multiply_reduce_fusion = f32[]{:T(128)} fusion(f32[32,256,128]{2,1,0:T(8,128)} %param.21), kind=kLoop, calls=%fused_computation.26 | loop fusion | flops 2097151 | bytes 4194308 | tf_op jit(solution)/shard_map/reduce_sum | solution.py:165
  56.2 2.9 %broadcast_add_fusion = f32[16,256,384]{2,1,0:T(8,128)} fusion(f32[16,256]{1,0:T(8,128)S(1)} %get-tuple-element.101, f32[384]{0:T(512)S(1)} %broadcast_multiply_fusion.2), kind=kLoop, calls=%fused_computation.33 | loop fusion | flops 1572864 | bytes 6309376 | tf_op jit(solution)/shard_map/add | solution.py:134
  59.1 1.5 all-to-all-done
  61.5 3.2 %multiply_bitcast_fusion = f32[16,256,384]{2,1,0:T(8,128)S(1)} fusion(f32[]{:T(128)} %bitcast.6, f32[1,16,384]{2,0,1:T(1,128)S(1)} %broadcast_in_dim.41, f32[7,16,384]{2,0,1:T(8,128)S(1)} %copy.133, f32[7,16,384]{2,0,1:T(8,128)S(1)} %copy.132, f32[8,256]{1,0:T(8,128)S(1)} %copy-done.9, f32[8,256]{1,0:T(8,128)S(1)} %gather_fusion), kind=kOutput, calls=%fused_computation.6 | convolution fusion | flops 152866816 | bytes 6676484 | tf_op jit(solution)/shard_map/rki,rj->kji/dot_general | solution.py:131
  64.7 3.7 %fusion.54 = f32[4,16,256]{2,0,1:T(4,128)S(1)} fusion(f32[16,256,384]{2,1,0:T(8,128)S(1)} %multiply_bitcast_fusion, f32[16,256]{1,0:T(8,128)S(1)} %get-tuple-element.101, f32[384]{0:T(512)S(1)} %broadcast_multiply_fusion.2, f32[16,4,256]{2,0,1:T(8,128)S(1)} %convolution_bitcast_fusion.3, f32[384,4]{0,1:T(4,128)S(1)} %copy-done.10, ...), kind=kOutput, calls=%fused_computation.57 | convolution fusion | flops 40913920 | bytes 6452740 | tf_op jit(solution)/shard_map/kji,iq->qkj/dot_general | solution.py:135
  68.4 9.0 %all-gather = f32[16,16,256]{2,1,0:T(8,128)S(1)} all-gather(f32[4,16,256]{2,1,0:T(8,128)S(1)} %copy.106), channel_id=2, replica_groups=mesh['blk'=4,'py'=4,'pz'=2] {'blk'}, dimensions={0}, use_global_device_ids=true | all-gather | bytes 327680 | tf_op jit(solution)/shard_map/all_gather | solution.py:139
  77.4 2.5 fusion.124
  79.9 2.5 fusion.125
  82.4 5.0 %multiply_add_fusion.36 = (f32[1,1,16,256]{3,2,1,0:T(8,128)S(1)}, f32[1,1,16,256]{3,2,1,0:T(8,128)S(1)}) fusion(f32[4,4,16,256]{3,2,1,0:T(8,128)S(1)} %bitcast.296, f32[]{:T(128)} %bitcast.31, f32[]{:T(128)} %bitcast.30, f32[]{:T(128)} %bitcast.29, f32[]{:T(128)} %bitcast.23, f32[]{:T(128)} %bitcast.53, f32[]{:T(128)} %bitcast.52, f32[]{:T(128)} %bitcast.51, ...), kind=kLoop, calls=%fused_computation.197 | loop fusion | flops 57344 | bytes 163872 | tf_op jit(solution)/shard_map/add | solution.py:59
  87.4 5.2 %multiply_add_fusion.35 = (f32[1,1,16,256]{3,2,1,0:T(8,128)S(1)}, f32[1,1,16,256]{3,2,1,0:T(8,128)S(1)}) fusion(f32[4,4,16,256]{3,2,1,0:T(8,128)S(1)} %bitcast.297, f32[]{:T(128)} %bitcast.36, f32[]{:T(128)} %bitcast.35, f32[]{:T(128)} %bitcast.34, f32[]{:T(128)} %bitcast.33, f32[]{:T(128)} %bitcast.57, f32[]{:T(128)} %bitcast.56, f32[]{:T(128)} %bitcast.55, ...), kind=kLoop, calls=%fused_computation.196 | loop fusion | flops 57344 | bytes 163872 | tf_op jit(solution)/shard_map/add | solution.py:59
  92.6 5.1 %multiply_add_fusion.34 = (f32[1,1,16,256]{3,2,1,0:T(8,128)S(1)}, f32[1,1,16,256]{3,2,1,0:T(8,128)S(1)}) fusion(f32[4,4,16,256]{3,2,1,0:T(8,128)S(1)} %bitcast.298, f32[]{:T(128)} %bitcast.41, f32[]{:T(128)} %bitcast.40, f32[]{:T(128)} %bitcast.39, f32[]{:T(128)} %bitcast.38, f32[]{:T(128)} %bitcast.61, f32[]{:T(128)} %bitcast.60, f32[]{:T(128)} %bitcast.59, ...), kind=kLoop, calls=%fused_computation.195 | loop fusion | flops 57344 | bytes 163872 | tf_op jit(solution)/shard_map/add | solution.py:59
  97.8 0.7 fusion.79
  98.5 5.1 %multiply_add_fusion.29 = (f32[1,16,256]{2,1,0:T(8,128)S(1)}, f32[1,16,256]{2,1,0:T(8,128)S(1)}) fusion(f32[4,16,256]{2,1,0:T(8,128)S(1)} %get-tuple-element.11, f32[]{:T(128)} %bitcast.31, f32[]{:T(128)} %bitcast.30, f32[]{:T(128)} %bitcast.29, f32[]{:T(128)} %bitcast.23, f32[]{:T(128)} %bitcast.36, f32[]{:T(128)} %bitcast.35, f32[]{:T(128)} %bitcast.34, ...), kind=kLoop, calls=%fused_computation.179 | loop fusion | flops 57344 | bytes 98336 | tf_op jit(solution)/shard_map/add | solution.py:59
  103.6 5.0 %multiply_add_fusion.27 = (f32[1,16,256]{2,1,0:T(8,128)S(1)}, f32[1,16,256]{2,1,0:T(8,128)S(1)}) fusion(f32[4,16,256]{2,1,0:T(8,128)S(1)} %get-tuple-element.11, f32[]{:T(128)} %bitcast.41, f32[]{:T(128)} %bitcast.40, f32[]{:T(128)} %bitcast.39, f32[]{:T(128)} %bitcast.38, f32[]{:T(128)} %bitcast.47, f32[]{:T(128)} %bitcast.45, f32[]{:T(128)} %bitcast.44, ...), kind=kLoop, calls=%fused_computation.177 | loop fusion | flops 57344 | bytes 98336 | tf_op jit(solution)/shard_map/add | solution.py:59
  108.7 5.0 %multiply_add_fusion.25 = (f32[1,16,256]{2,1,0:T(8,128)S(1)}, f32[1,16,256]{2,1,0:T(8,128)S(1)}) fusion(f32[4,16,256]{2,1,0:T(8,128)S(1)} %get-tuple-element.54, f32[]{:T(128)} %bitcast.53, f32[]{:T(128)} %bitcast.52, f32[]{:T(128)} %bitcast.51, f32[]{:T(128)} %bitcast.50, f32[]{:T(128)} %bitcast.57, f32[]{:T(128)} %bitcast.56, f32[]{:T(128)} %bitcast.55, ...), kind=kLoop, calls=%fused_computation.175 | loop fusion | flops 57344 | bytes 98336 | tf_op jit(solution)/shard_map/add | solution.py:59
  113.7 5.0 %multiply_add_fusion.23 = (f32[1,16,256]{2,1,0:T(8,128)S(1)}, f32[1,16,256]{2,1,0:T(8,128)S(1)}) fusion(f32[4,16,256]{2,1,0:T(8,128)S(1)} %get-tuple-element.54, f32[]{:T(128)} %bitcast.61, f32[]{:T(128)} %bitcast.60, f32[]{:T(128)} %bitcast.59, f32[]{:T(128)} %bitcast.58, f32[]{:T(128)} %bitcast.65, f32[]{:T(128)} %bitcast.64, f32[]{:T(128)} %bitcast.63, ...), kind=kLoop, calls=%fused_computation.173 | loop fusion | flops 57344 | bytes 98336 | tf_op jit(solution)/shard_map/add | solution.py:59
  118.8 5.0 %multiply_add_fusion.17 = (f32[1,16,256]{2,1,0:T(8,128)S(1)}, f32[1,16,256]{2,1,0:T(8,128)S(1)}) fusion(f32[4,16,256]{2,1,0:T(8,128)S(1)} %get-tuple-element.55, f32[]{:T(128)} %bitcast.53, f32[]{:T(128)} %bitcast.52, f32[]{:T(128)} %bitcast.51, f32[]{:T(128)} %bitcast.50, f32[]{:T(128)} %bitcast.57, f32[]{:T(128)} %bitcast.56, f32[]{:T(128)} %bitcast.55, ...), kind=kLoop, calls=%fused_computation.167 | loop fusion | flops 57344 | bytes 98336 | tf_op jit(solution)/shard_map/add | solution.py:59
  123.8 5.0 %multiply_add_fusion.15 = (f32[1,16,256]{2,1,0:T(8,128)S(1)}, f32[1,16,256]{2,1,0:T(8,128)S(1)}) fusion(f32[4,16,256]{2,1,0:T(8,128)S(1)} %get-tuple-element.55, f32[]{:T(128)} %bitcast.61, f32[]{:T(128)} %bitcast.60, f32[]{:T(128)} %bitcast.59, f32[]{:T(128)} %bitcast.58, f32[]{:T(128)} %bitcast.65, f32[]{:T(128)} %bitcast.64, f32[]{:T(128)} %bitcast.63, ...), kind=kLoop, calls=%fused_computation.165 | loop fusion | flops 57344 | bytes 98336 | tf_op jit(solution)/shard_map/add | solution.py:59
  128.9 5.1 %multiply_add_fusion.21 = (f32[1,16,256]{2,1,0:T(8,128)S(1)}, f32[1,16,256]{2,1,0:T(8,128)S(1)}) fusion(f32[4,16,256]{2,1,0:T(8,128)S(1)} %get-tuple-element.10, f32[]{:T(128)} %bitcast.31, f32[]{:T(128)} %bitcast.30, f32[]{:T(128)} %bitcast.29, f32[]{:T(128)} %bitcast.23, f32[]{:T(128)} %bitcast.36, f32[]{:T(128)} %bitcast.35, f32[]{:T(128)} %bitcast.34, ...), kind=kLoop, calls=%fused_computation.171 | loop fusion | flops 57344 | bytes 98336 | tf_op jit(solution)/shard_map/add | solution.py:59
  134.0 5.0 %multiply_add_fusion.19 = (f32[1,16,256]{2,1,0:T(8,128)S(1)}, f32[1,16,256]{2,1,0:T(8,128)S(1)}) fusion(f32[4,16,256]{2,1,0:T(8,128)S(1)} %get-tuple-element.10, f32[]{:T(128)} %bitcast.41, f32[]{:T(128)} %bitcast.40, f32[]{:T(128)} %bitcast.39, f32[]{:T(128)} %bitcast.38, f32[]{:T(128)} %bitcast.47, f32[]{:T(128)} %bitcast.45, f32[]{:T(128)} %bitcast.44, ...), kind=kLoop, calls=%fused_computation.169 | loop fusion | flops 57344 | bytes 98336 | tf_op jit(solution)/shard_map/add | solution.py:59
  139.2 5.1 %multiply_add_fusion.13 = (f32[1,16,256]{2,1,0:T(8,128)S(1)}, f32[1,16,256]{2,1,0:T(8,128)S(1)}) fusion(f32[4,16,256]{2,1,0:T(8,128)S(1)} %multiply_add_fusion.3, f32[]{:T(128)} %bitcast.31, f32[]{:T(128)} %bitcast.30, f32[]{:T(128)} %bitcast.29, f32[]{:T(128)} %bitcast.23, f32[]{:T(128)} %bitcast.36, f32[]{:T(128)} %bitcast.35, f32[]{:T(128)} %bitcast.34, ...), kind=kLoop, calls=%fused_computation.163 | loop fusion | flops 57344 | bytes 98336 | tf_op jit(solution)/shard_map/add | solution.py:59
  144.3 5.0 %multiply_add_fusion.11 = (f32[1,16,256]{2,1,0:T(8,128)S(1)}, f32[1,16,256]{2,1,0:T(8,128)S(1)}) fusion(f32[4,16,256]{2,1,0:T(8,128)S(1)} %multiply_add_fusion.3, f32[]{:T(128)} %bitcast.41, f32[]{:T(128)} %bitcast.40, f32[]{:T(128)} %bitcast.39, f32[]{:T(128)} %bitcast.38, f32[]{:T(128)} %bitcast.47, f32[]{:T(128)} %bitcast.45, f32[]{:T(128)} %bitcast.44, ...), kind=kLoop, calls=%fused_computation.161 | loop fusion | flops 57344 | bytes 98336 | tf_op jit(solution)/shard_map/add | solution.py:59
  149.4 5.0 %multiply_add_fusion.9 = (f32[1,16,256]{2,1,0:T(8,128)S(1)}, f32[1,16,256]{2,1,0:T(8,128)S(1)}) fusion(f32[4,16,256]{2,1,0:T(8,128)S(1)} %get-tuple-element.6, f32[]{:T(128)} %bitcast.53, f32[]{:T(128)} %bitcast.52, f32[]{:T(128)} %bitcast.51, f32[]{:T(128)} %bitcast.50, f32[]{:T(128)} %bitcast.57, f32[]{:T(128)} %bitcast.56, f32[]{:T(128)} %bitcast.55, ...), kind=kLoop, calls=%fused_computation.159 | loop fusion | flops 57344 | bytes 98336 | tf_op jit(solution)/shard_map/add | solution.py:59
  154.4 5.0 %multiply_add_fusion.7 = (f32[1,16,256]{2,1,0:T(8,128)S(1)}, f32[1,16,256]{2,1,0:T(8,128)S(1)}) fusion(f32[4,16,256]{2,1,0:T(8,128)S(1)} %get-tuple-element.6, f32[]{:T(128)} %bitcast.61, f32[]{:T(128)} %bitcast.60, f32[]{:T(128)} %bitcast.59, f32[]{:T(128)} %bitcast.58, f32[]{:T(128)} %bitcast.65, f32[]{:T(128)} %bitcast.64, f32[]{:T(128)} %bitcast.63, ...), kind=kLoop, calls=%fused_computation.157 | loop fusion | flops 57344 | bytes 98336 | tf_op jit(solution)/shard_map/add | solution.py:59
  159.4 0.7 select_reduce_fusion.1
  160.1 5.1 %add_bitcast_fusion.7 = (f32[1,1,16,256]{3,2,1,0:T(8,128)S(1)}, f32[1,1,16,256]{3,2,1,0:T(8,128)S(1)}) fusion(f32[4,16,256]{2,1,0:T(8,128)S(1)} %get-tuple-element.4, f32[]{:T(128)} %bitcast.31, f32[]{:T(128)} %bitcast.30, f32[]{:T(128)} %bitcast.29, f32[]{:T(128)} %bitcast.23, f32[]{:T(128)} %bitcast.36, f32[]{:T(128)} %bitcast.35, f32[]{:T(128)} %bitcast.34, ...), kind=kLoop, calls=%fused_computation.155 | loop fusion | flops 57344 | bytes 98336 | tf_op jit(solution)/shard_map/stack | solution.py:61
  165.3 5.0 %add_bitcast_fusion.5 = (f32[1,1,16,256]{3,2,1,0:T(8,128)S(1)}, f32[1,1,16,256]{3,2,1,0:T(8,128)S(1)}) fusion(f32[4,16,256]{2,1,0:T(8,128)S(1)} %get-tuple-element.4, f32[]{:T(128)} %bitcast.41, f32[]{:T(128)} %bitcast.40, f32[]{:T(128)} %bitcast.39, f32[]{:T(128)} %bitcast.38, f32[]{:T(128)} %bitcast.47, f32[]{:T(128)} %bitcast.45, f32[]{:T(128)} %bitcast.44, ...), kind=kLoop, calls=%fused_computation.153 | loop fusion | flops 57344 | bytes 98336 | tf_op jit(solution)/shard_map/stack | solution.py:61
  170.4 5.0 %add_bitcast_fusion.3 = (f32[1,1,16,256]{3,2,1,0:T(8,128)S(1)}, f32[1,1,16,256]{3,2,1,0:T(8,128)S(1)}) fusion(f32[4,16,256]{2,1,0:T(8,128)S(1)} %get-tuple-element.5, f32[]{:T(128)} %bitcast.53, f32[]{:T(128)} %bitcast.52, f32[]{:T(128)} %bitcast.51, f32[]{:T(128)} %bitcast.50, f32[]{:T(128)} %bitcast.57, f32[]{:T(128)} %bitcast.56, f32[]{:T(128)} %bitcast.55, ...), kind=kLoop, calls=%fused_computation.151 | loop fusion | flops 57344 | bytes 98336 | tf_op jit(solution)/shard_map/stack | solution.py:61
  175.4 5.0 %add_bitcast_fusion.1 = (f32[1,1,16,256]{3,2,1,0:T(8,128)S(1)}, f32[1,1,16,256]{3,2,1,0:T(8,128)S(1)}) fusion(f32[4,16,256]{2,1,0:T(8,128)S(1)} %get-tuple-element.5, f32[]{:T(128)} %bitcast.61, f32[]{:T(128)} %bitcast.60, f32[]{:T(128)} %bitcast.59, f32[]{:T(128)} %bitcast.58, f32[]{:T(128)} %bitcast.65, f32[]{:T(128)} %bitcast.64, f32[]{:T(128)} %bitcast.63, ...), kind=kLoop, calls=%fused_computation.149 | loop fusion | flops 57344 | bytes 98336 | tf_op jit(solution)/shard_map/stack | solution.py:61
  180.4 2.4 bitcast_add_fusion.3
  182.9 2.5 multiply_add_fusion.30
  185.4 0.8 multiply_add_fusion.1
  186.2 0.8 multiply_add_fusion
  187.0 0.7 fusion.71
  187.8 0.7 convolution_bitcast_fusion.1
  189.8 5.2 %fusion.47 = f32[8,16,2,256]{3,0,1,2:T(8,128)S(1)} fusion(f32[8,2,256,1]{2,0,3,1:T(8,128)S(1)} %copy-done.19, f32[16,256,384]{2,1,0:T(8,128)} %broadcast_add_fusion, f32[16,256,384]{2,1,0:T(8,128)} %copy-done.1, f32[256]{0:T(256)S(1)} %copy-done.22, f32[16,256]{1,0:T(8,128)S(1)} %get-tuple-element.67, f32[256]{0:T(256)S(1)} %copy-done.21, ...), kind=kOutput, calls=%fused_computation.51 | convolution fusion | flops 106037248 | bytes 9095168 | tf_op jit(solution)/shard_map/kji,dsj->dksi/dot_general | solution.py:198
  195.7 0.8 pad_maximum_fusion.1
  196.4 3.6 %all-to-all-start.1 = ((f32[8,16,576]{2,1,0:T(8,128)}), f32[8,16,576]{2,1,0:T(8,128)S(1)}, u32[]{:S(2)}, u32[]{:S(2)}) async-start(f32[8,16,576]{2,1,0:T(8,128)} %pad_maximum_fusion.1), calls=%async_computation.1 | async-start | bytes 655360 | tf_op jit(solution)/shard_map/all_to_all | solution.py:210
  200.0 0.7 pad_maximum_fusion.3
  200.7 0.6 multiply_bitcast_fusion.1
  201.3 40.1 %psum.7 = f32[3]{0:T(128)S(1)} all-reduce(f32[3]{0:T(128)S(1)} %pad_maximum_fusion.3), channel_id=1, replica_groups=mesh['blk'=4,'py'=4,'pz'=2] {'blk','py','pz'}, use_global_device_ids=true, to_apply=%region_5.6 | all-reduce | flops 3 | bytes 24 | tf_op jit(solution)/shard_map/psum | solution.py:233
  242.4 6.3 %fusion.6 = f32[32,256,128]{2,0,1:T(8,128)S(1)} fusion(f32[32,32,1]{1,0,2:T(8,128)S(1)} %copy-done.8, f32[32,384,128]{2,0,1:T(8,128)} %get-tuple-element.29, f32[32,384,128]{2,0,1:T(8,128)} %get-tuple-element.112, f32[32,128]{1,0:T(8,128)S(1)} %get-tuple-element.65, f32[256]{0:T(256)S(1)} %copy-done.22, f32[32,128]{1,0:T(8,128)S(1)} %get-tuple-element.64, ...), kind=kOutput, calls=%fused_computation.10 | convolution fusion | flops 210763776 | bytes 12884224 | tf_op jit(solution)/shard_map/mik,ym->yik/dot_general | solution.py:228
  248.8 4.3 %fusion.20 = f32[256,32,128]{2,0,1:T(8,128)S(1)} fusion(f32[32,256,128]{2,0,1:T(8,128)S(1)} %fusion.6, f32[256,256]{1,0:T(8,128)S(1)} %copy-done.7, f32[256,256]{1,0:T(8,128)S(1)} %copy-done.3, pred[]{:T(512)S(6)} %eq.32), kind=kOutput, calls=%fused_computation.24 | convolution fusion | flops 1610678272 | bytes 8912897 | tf_op jit(solution)/shard_map/yik,pi->ypk/dot_general | solution.py:229
  253.1 3.3 %fusion.16 = f32[32,256,128]{2,1,0:T(8,128)} fusion(f32[128,128,1]{0,1,2:T(8,128)S(1)} %copy-done.6, f32[256,32,128]{2,0,1:T(8,128)S(1)} %fusion.20), kind=kOutput, calls=%fused_computation.20 | convolution fusion | flops 805306368 | bytes 8454144 | tf_op jit(solution)/shard_map/ypk,zk->ypz/dot_general | solution.py:230
  (89 shorter events, 4.1 us)
Async XLA Ops:
  4.0 4.2 %copy-start.4 = (f32[256,384]{0,1:T(8,128)S(1)}, f32[256,384]{0,1:T(8,128)}, u32[]{:S(2)}) copy-start(f32[256,384]{0,1:T(8,128)} %constant.105) | copy-start | bytes 1179652
  4.0 4.2 %copy-start.5 = (f32[256,384]{0,1:T(8,128)S(1)}, f32[256,384]{0,1:T(8,128)}, u32[]{:S(2)}) copy-start(f32[256,384]{0,1:T(8,128)} %constant.93.clone) | copy-start | bytes 1179652
  8.3 3.1 %copy-start.13 = (f32[384]{0:T(512)S(1)}, f32[384]{0:T(512)}, u32[]{:S(2)}) copy-start(f32[384]{0:T(512)} %constant.92.clone) | copy-start | bytes 4612
  8.3 3.8 %copy-start.20 = (f32[32]{0:T(128)S(1)}, f32[32]{0:T(128)}, u32[]{:S(2)}) copy-start(f32[32]{0:T(128)} %constant.90.clone) | copy-start | bytes 388
  8.3 4.5 %copy-start.18 = (f32[128]{0:T(128)S(1)}, f32[128]{0:T(128)}, u32[]{:S(2)}) copy-start(f32[128]{0:T(128)} %constant.91.clone) | copy-start | bytes 1540
  8.3 5.2 %copy-start.8 = (f32[32,32,1]{1,0,2:T(8,128)S(1)}, f32[32,32,1]{1,0,2:T(8,128)}, u32[]{:S(2)}) copy-start(f32[32,32,1]{1,0,2:T(8,128)} %constant.115) | copy-start | bytes 12292
  13.5 14.4 %copy-start.10 = (f32[384,4]{0,1:T(4,128)S(1)}, f32[384,4]{0,1:T(4,128)}, u32[]{:S(2)}) copy-start(f32[384,4]{0,1:T(4,128)} %constant.94.clone) | copy-start | bytes 18436
  13.5 14.3 %copy-start.11 = (f32[384,4]{0,1:T(4,128)S(1)}, f32[384,4]{0,1:T(4,128)}, u32[]{:S(2)}) copy-start(f32[384,4]{0,1:T(4,128)} %constant.95.clone) | copy-start | bytes 18436
  25.3 2.6 %copy-start = (f32[32,384,128]{2,0,1:T(8,128)}, f32[32,384,128]{2,0,1:T(8,128)S(1)}, u32[]{:S(2)}) copy-start(f32[32,384,128]{2,0,1:T(8,128)S(1)} %get-tuple-element.28) | copy-start | bytes 18874372
  25.3 8.6 %copy-start.12 = (f32[32,32]{1,0:T(8,128)S(1)}, f32[32,32]{1,0:T(8,128)}, u32[]{:S(2)}) copy-start(f32[32,32]{1,0:T(8,128)} %constant.86.clone) | copy-start | bytes 12292
  34.4 13.1 %copy-start.15 = (f32[256]{0:T(256)S(1)}, f32[256]{0:T(256)}, u32[]{:S(2)}) copy-start(f32[256]{0:T(256)} %constant.89.clone) | copy-start | bytes 3076
  34.4 13.6 %copy-start.14 = (s32[4,2]{0,1:T(2,128)S(1)}, s32[4,2]{0,1:T(2,128)}, u32[]{:S(2)}) copy-start(s32[4,2]{0,1:T(2,128)} %param.23) | copy-start | bytes 100
  34.5 16.6 %copy-start.3 = (f32[256,256]{1,0:T(8,128)S(1)}, f32[256,256]{1,0:T(8,128)}, u32[]{:S(2)}) copy-start(f32[256,256]{1,0:T(8,128)} %constant.85.clone) | copy-start | bytes 786436
  40.4 20.3 %all-to-all-start = ((f32[8,16,896]{2,1,0:T(8,128)}), f32[8,16,896]{2,1,0:T(8,128)S(1)}, u32[]{:S(2)}, u32[]{:S(2)}) async-start(f32[8,16,896]{2,1,0:T(8,128)} %pad_maximum_fusion), calls=%async_computation | async-start | bytes 917504 | tf_op jit(solution)/shard_map/all_to_all | solution.py:118
  56.2 4.8 %copy-start.2 = (f32[8,32,256,1]{2,1,0,3:T(8,128)S(1)}, f32[8,32,256,1]{2,1,0,3:T(8,128)}, u32[]{:S(2)}) copy-start(f32[8,32,256,1]{2,1,0,3:T(8,128)} %constant.117) | copy-start | bytes 786436
  56.2 5.2 %copy-start.9 = (f32[8,256]{1,0:T(8,128)S(1)}, f32[8,256]{1,0:T(8,128)}, u32[]{:S(2)}) copy-start(f32[8,256]{1,0:T(8,128)} %constant.108) | copy-start | bytes 24580
  64.7 3.7 %copy-start.1 = (f32[16,256,384]{2,1,0:T(8,128)}, f32[16,256,384]{2,1,0:T(8,128)S(1)}, u32[]{:S(2)}) copy-start(f32[16,256,384]{2,1,0:T(8,128)S(1)} %multiply_bitcast_fusion) | copy-start | bytes 18874372
  92.6 97.1 %copy-start.19 = (f32[8,2,256,1]{2,0,3,1:T(8,128)S(1)}, f32[8,2,256,1]{2,0,3,1:T(8,128)}, u32[]{:S(2)}) copy-start(f32[8,2,256,1]{2,0,3,1:T(8,128)} %constant.118) | copy-start | bytes 49156
  92.6 97.1 %copy-start.21 = (f32[256]{0:T(256)S(1)}, f32[256]{0:T(256)}, u32[]{:S(2)}) copy-start(f32[256]{0:T(256)} %constant.111) | copy-start | bytes 3076
  92.6 97.1 %copy-start.22 = (f32[256]{0:T(256)S(1)}, f32[256]{0:T(256)}, u32[]{:S(2)}) copy-start(f32[256]{0:T(256)} %constant.113) | copy-start | bytes 3076
  189.7 10.9 %copy-start.16 = (f32[1,32]{1,0:T(1,128)S(1)}, f32[1,32]{1,0:T(1,128)}, u32[]{:S(2)}) copy-start(f32[1,32]{1,0:T(1,128)} %constant.106) | copy-start | bytes 388
  189.7 10.9 %copy-start.17 = (f32[1,32]{1,0:T(1,128)S(1)}, f32[1,32]{1,0:T(1,128)}, u32[]{:S(2)}) copy-start(f32[1,32]{1,0:T(1,128)} %constant.114) | copy-start | bytes 388
  196.4 45.4 %all-to-all-start.1 = ((f32[8,16,576]{2,1,0:T(8,128)}), f32[8,16,576]{2,1,0:T(8,128)S(1)}, u32[]{:S(2)}, u32[]{:S(2)}) async-start(f32[8,16,576]{2,1,0:T(8,128)} %pad_maximum_fusion.1), calls=%async_computation.1 | async-start | bytes 655360 | tf_op jit(solution)/shard_map/all_to_all | solution.py:210
  242.4 6.3 %copy-start.7 = (f32[256,256]{1,0:T(8,128)S(1)}, f32[256,256]{1,0:T(8,128)}, u32[]{:S(2)}) copy-start(f32[256,256]{1,0:T(8,128)} %constant.104) | copy-start | bytes 786436
  248.8 4.3 %copy-start.6 = (f32[128,128,1]{0,1,2:T(8,128)S(1)}, f32[128,128,1]{0,1,2:T(8,128)}, u32[]{:S(2)}) copy-start(f32[128,128,1]{0,1,2:T(8,128)} %constant.116) | copy-start | bytes 196612

commit v2 on v1

--- a/solution.py
+++ b/solution.py
@@ -1,7 +1,10 @@
+import functools
 import jax
 import jax.numpy as jnp
 import numpy as np
 from jax import lax
+from jax.experimental import pallas as pl
+from jax.experimental.pallas import tpu as pltpu
 from jax.sharding import PartitionSpec as P
 
 OV = 64
@@ -49,16 +52,73 @@
     return own, forward, mu, box_pick, margin_pick
 
 
-def shift_blocks(values, ids):
-    blocks = ids.shape[0]
-    match = (ids[:, None] == jnp.arange(blocks, dtype=jnp.int32)[None, :]).astype(jnp.float32)
-    rows = []
-    for b in range(blocks):
-        total = match[b, 0] * values[0]
-        for other in range(1, blocks):
-            total = total + match[b, other] * values[other]
-        rows.append(total)
-    return jnp.stack(rows)
+def chain_kernel(planes, ids_ref, own_ref, c0_ref, theta_ref, sinh_ref, every_ref, push_ref, square_ref):
+    blocks = every_ref.shape[0]
+    c0 = c0_ref[0]
+    theta = theta_ref[...]
+    sinh = sinh_ref[...]
+    far = jnp.exp(-2.0 * OV * theta)
+    outer = (1.0 + far) / (1.0 - far)
+    reach = jnp.exp(-(planes + 1.0) * theta)
+    mid = (1.0 - reach) / (1.0 + reach)
+    even_inv = 1.0 / (sinh * (outer + mid))
+    odd_inv = 1.0 / (sinh * (outer + 1.0 / mid))
+    span = 1.0 - reach * reach
+    beta = 2.0 * sinh * reach / span
+    alpha = jnp.exp(-theta) * (1.0 - jnp.exp(-2.0 * planes * theta)) / span
+    masks = [
+        [[(ids_ref[b, side] == o).astype(jnp.float32) for o in range(blocks)] for b in range(blocks)]
+        for side in range(2)
+    ]
+    mine = [(own_ref[0] == b).astype(jnp.float32) for b in range(blocks)]
+
+    def beside(values, side):
+        shifted = []
+        for b in range(blocks):
+            total = masks[side][b][0] * values[0]
+            for o in range(1, blocks):
+                total = total + masks[side][b][o] * values[o]
+            shifted.append(total)
+        return shifted
+
+    each = range(blocks)
+    own_low = [every_ref[b, 0] for b in each]
+    own_high = [every_ref[b, 1] for b in each]
+    beyond_low = [v / c0 for v in beside([every_ref[b, 2] for b in each], 0)]
+    beyond_high = [v / c0 for v in beside([every_ref[b, 3] for b in each], 1)]
+    push_low = jnp.zeros_like(theta)
+    push_high = jnp.zeros_like(theta)
+    for iteration in range(ITERS):
+        lows, highs, inner_lows, inner_highs = [], [], [], []
+        for b in each:
+            drive_low = beyond_low[b] + own_low[b]
+            drive_high = beyond_high[b] + own_high[b]
+            even = (drive_low + drive_high) * even_inv
+            odd = (drive_low - drive_high) * odd_inv
+            low = 0.5 * (even + odd)
+            high = 0.5 * (even - odd)
+            push_low = push_low + mine[b] * low
+            push_high = push_high + mine[b] * high
+            lows.append(low)
+            highs.append(high)
+            inner_lows.append(own_low[b] + alpha * low + beta * high)
+            inner_highs.append(own_high[b] + beta * low + alpha * high)
+        if iteration == ITERS - 1:
+            break
+        jump_low = [v - low for v, low in zip(beside(inner_highs, 0), lows)]
+        jump_high = [v - high for v, high in zip(beside(inner_lows, 1), highs)]
+        square = jnp.zeros_like(theta)
+        for b in each:
+            square = square + jump_low[b] * jump_low[b] + jump_high[b] * jump_high[b]
+            push_low = push_low + mine[b] * jump_low[b]
+            push_high = push_high + mine[b] * jump_high[b]
+        square_ref[iteration] = square
+        own_low = [alpha * jump_low[b] + beta * jump_high[b] for b in each]
+        own_high = [beta * jump_low[b] + alpha * jump_high[b] for b in each]
+        beyond_low = beside(jump_high, 0)
+        beyond_high = beside(jump_low, 1)
+    push_ref[0] = c0 * push_low
+    push_ref[1] = c0 * push_high
 
 
 def shards(source, conduct, neighbours, orient):
@@ -99,26 +159,36 @@
     pick = jnp.asarray(box_pick) + c0 * jnp.asarray(margin_pick)
 
     cells = jnp.einsum("ypz,zk->ypk", source, depth_basis, precision=HIGH)
-    cells = jnp.einsum("ypk,pi->yik", cells, forward, precision=HIGH)
-    modes = jnp.einsum("yik,ym->mik", cells, local_basis, precision=HIGH)
+    cells = jnp.einsum("ypk,ym->mpk", cells, local_basis, precision=HIGH)
+    modes = jnp.einsum("mpk,pi->mik", cells, forward, precision=HIGH)
     slab_spectra = (
         c0 * mu_plane[None, :, None]
         + c1 * mu_local[:, None, None]
         + c2 * mu_depth[None, None, :]
     )
     slab = modes / slab_spectra
-    edges = jnp.einsum("mik,em->eki", slab, local_basis[jnp.array([0, rows - 1])], precision=HIGH)
-    ends = jnp.einsum("mik,iq->mqk", slab, pick, precision=HIGH)
-    ends = jnp.einsum("mqk,ym->kqy", ends, local_basis, precision=HIGH)
-    plain = jnp.zeros((2, rows, depth), jnp.float32)
-    plain = jnp.concatenate([plain, jnp.stack([cells[:, count - 2], cells[:, count - 1]])], axis=0)
-    ends = ends + jnp.transpose(plain, (2, 0, 1))
-
-    packed = jnp.concatenate([edges[0], edges[1], ends.reshape(depth, 4 * rows)], axis=1)
+    edge_first = jnp.sum(slab * local_basis[0][:, None, None], axis=0)
+    edge_last = jnp.sum(slab * local_basis[-1][:, None, None], axis=0)
+    ends = jnp.einsum("mik,iq->mqk", slab, pick, precision=HIGHEST)
+    plain = jnp.zeros((rows, 2, depth), jnp.float32)
+    ends = ends + jnp.concatenate([plain, modes[:, count - 2 :]], axis=1)
+    ends = jnp.einsum("mqk,ym->kqy", ends, local_basis, precision=HIGHEST)
+    own_squares = jnp.sum(source * source)
+
+    packed = jnp.concatenate(
+        [
+            jnp.transpose(edge_first),
+            jnp.transpose(edge_last)[:, : count - 1],
+            jnp.full((depth, 1), own_squares),
+            ends.reshape(depth, 4 * rows),
+        ],
+        axis=1,
+    )
     packed = lax.all_to_all(packed, ("py", "pz"), split_axis=0, concat_axis=0, tiled=True)
     packed = packed.reshape(group, own_depth, 2 * count + 4 * rows)
     edge_first = packed[:, :, :count]
     edge_last = packed[:, :, count : 2 * count]
+    first_square = jnp.sum(packed[:, 0, 2 * count - 1])
     ends = packed[:, :, 2 * count :].reshape(group, own_depth, 4, rows)
 
     empty = jnp.zeros_like(edge_first[:1])
@@ -128,66 +198,34 @@
     last_rows = row_basis[rows * np.arange(group) + rows - 1]
     seam_basis = jnp.concatenate([first_rows, last_rows], axis=0)
     seams = jnp.concatenate([below, above], axis=0)
-    joined = c1 * jnp.einsum("rki,rj->kji", seams, seam_basis, precision=HIGH)
+    joined = c1 * jnp.einsum("rki,rj->kji", seams, seam_basis, precision=HIGHEST)
     held_depth = lax.dynamic_slice_in_dim(mu_depth, member * own_depth, own_depth)
     cross = c1 * mu_row[None, :] + c2 * held_depth[:, None]
     spectra = c0 * mu_plane[None, None, :] + cross[:, :, None]
-    moments = jnp.einsum("kji,iq->qkj", joined / spectra, pick, precision=HIGH)
+    moments = jnp.einsum("kji,iq->qkj", joined / spectra, pick, precision=HIGHEST)
     moments = moments + jnp.einsum(
         "dkqy,dyj->qkj", ends, row_basis.reshape(group, rows, all_rows), precision=HIGHEST
     )
-    every = lax.all_gather(moments, "blk", axis=0)
+    shared = jnp.full((1,) + moments.shape[1:], first_square)
+    every = lax.all_gather(jnp.concatenate([moments, shared], axis=0), "blk", axis=0)
 
     half = 0.5 * jnp.sqrt(cross / c0)
     root = jnp.sqrt(1.0 + half * half)
     theta = 2.0 * jnp.log1p(half + half * half / (1.0 + root))
     sinh = 2.0 * half * root
-
-    def tanh_of(n):
-        decay = jnp.exp(-2.0 * n * theta)
-        return -jnp.expm1(-2.0 * n * theta) / (1.0 + decay)
-
-    outer = 1.0 / tanh_of(float(OV))
-    mid = tanh_of(0.5 * (planes + 1))
-    even_inv = 1.0 / (sinh * (outer + mid))
-    odd_inv = 1.0 / (sinh * (outer + 1.0 / mid))
-    reach = jnp.exp(-(planes + 1.0) * theta)
-    span = -jnp.expm1(-2.0 * (planes + 1.0) * theta)
-    beta = sinh * 2.0 * reach / span
-    alpha = jnp.exp(-theta) * -jnp.expm1(-2.0 * planes * theta) / span
-
-    left_ids, right_ids = neighbours[:, 0], neighbours[:, 1]
-    own_low, own_high = every[:, 0], every[:, 1]
-    beyond_low = shift_blocks(every[:, 2], left_ids) / c0
-    beyond_high = shift_blocks(every[:, 3], right_ids) / c0
-    push_low = jnp.zeros_like(own_low)
-    push_high = jnp.zeros_like(own_low)
-    squares = [jnp.sum(source * source)]
-    for iteration in range(ITERS):
-        drive_low = beyond_low + own_low
-        drive_high = beyond_high + own_high
-        even = (drive_low + drive_high) * even_inv
-        odd = (drive_low - drive_high) * odd_inv
-        low = 0.5 * (even + odd)
-        high = 0.5 * (even - odd)
-        push_low = push_low + low
-        push_high = push_high + high
-        if iteration == ITERS - 1:
-            break
-        inner_low = own_low + alpha * low + beta * high
-        inner_high = own_high + beta * low + alpha * high
-        jump_low = shift_blocks(inner_high, left_ids) - low
-        jump_high = shift_blocks(inner_low, right_ids) - high
-        held = jnp.where(chosen[:, None, None], jump_low**2 + jump_high**2, 0.0)
-        squares.append(c0 * c0 * jnp.sum(held))
-        push_low = push_low + jump_low
-        push_high = push_high + jump_high
-        own_low = alpha * jump_low + beta * jump_high
-        own_high = beta * jump_low + alpha * jump_high
-        beyond_low = shift_blocks(jump_high, left_ids)
-        beyond_high = shift_blocks(jump_low, right_ids)
-    pushes = c0 * jnp.stack([push_low, push_high], axis=1)
-    pushes = jnp.sum(jnp.where(chosen[:, None, None, None], pushes, 0.0), axis=0)
+    in_smem = pl.BlockSpec(memory_space=pltpu.SMEM)
+    in_vmem = pl.BlockSpec(memory_space=pltpu.VMEM)
+    pushes, squares = pl.pallas_call(
+        functools.partial(chain_kernel, planes),
+        out_shape=(
+            jax.ShapeDtypeStruct((2,) + theta.shape, jnp.float32),
+            jax.ShapeDtypeStruct((ITERS - 1,) + theta.shape, jnp.float32),
+        ),
+        in_specs=[in_smem, in_smem, in_smem, in_vmem, in_vmem, in_vmem],
+        out_specs=(in_vmem, in_vmem),
+        name="chain",
+    )(neighbours, own_block.reshape(1), c0.reshape(1), theta, sinh, every)
+    squares = c0 * c0 * jnp.sum(squares, axis=(1, 2))
 
     total = (
         joined[:, :, :planes]
@@ -195,7 +233,7 @@
         + pushes[1][:, :, None] * last_col
     )
     total = total / spectra[:, :, :planes]
-    beside_values = jnp.einsum("kji,dsj->dksi", total, beside_basis, precision=HIGH)
+    beside_values = jnp.einsum("kji,dsj->dksi", total, beside_basis, precision=HIGHEST)
     beside_values = beside_values + jnp.stack([below, above], axis=2)[:, :, :, :planes]
     pushes = jnp.einsum(
         "skj,dyj->dksy", pushes, row_basis.reshape(group, rows, all_rows), precision=HIGHEST
@@ -204,16 +242,18 @@
         [
             beside_values.reshape(group, own_depth, 2 * planes),
             pushes.reshape(group, own_depth, 2 * rows),
+            jnp.broadcast_to(squares, (group, own_depth, ITERS - 1)),
         ],
         axis=2,
-    ).reshape(depth, 2 * planes + 2 * rows)
+    ).reshape(depth, 2 * planes + 2 * rows + ITERS - 1)
     packed = lax.all_to_all(packed, ("py", "pz"), split_axis=0, concat_axis=0, tiled=True)
+    squares = packed[::own_depth, 2 * planes + 2 * rows :]
     packed = jnp.transpose(packed)
     below = packed[:planes]
     above = packed[planes : 2 * planes]
     pushes = jnp.einsum(
         "syk,ym->smk",
-        packed[2 * planes :].reshape(2, rows, depth),
+        packed[2 * planes : 2 * planes + 2 * rows].reshape(2, rows, depth),
         local_basis,
         precision=HIGHEST,
     )
@@ -230,7 +270,7 @@
     solution = jnp.einsum("ypk,zk->ypz", cells, depth_basis, precision=HIGH)
 
     cell_count = float(blocks * planes * all_rows * depth)
-    sums = lax.psum(jnp.stack(squares), ("blk", "py", "pz"))
+    sums = jnp.concatenate([jnp.sum(every[:, 4, 0, 0])[None], jnp.sum(squares, axis=0)])
     return (solution, jnp.sqrt(sums / cell_count))
 
 

time: 259 us -> 136 us (0.53)
  other arithmetic: 126 us -> 23.4 us
  blocking collectives: 49.1 us -> 9.98 us
  waiting for transfers between devices: 1.52 us -> 14.8 us
  local copies, waits for them, and re-layouts: 8.93 us -> 12.5 us
  Pallas kernels: 0 us -> 2.67 us
    add x26 -> x1, other arithmetic: 88.4 us -> 1.36 us  [shards(): cross = c1 * mu_row[None, :] + c2 * held_depth[:, None]]
    psum x1 -> x0, blocking collectives: 40.1 us -> none  [shards(): sums = lax.psum(jnp.stack(squares), ('blk', 'py', 'pz'))]
    another operation x6 -> x1, other arithmetic: 20.9 us -> 0.01 us  [the longest x4 20.2 us: shift_blocks(): return jnp.stack(rows)]
    all_to_all x2, waiting for transfers between devices: 1.52 us -> 14.8 us  [shards(): lax.all_to_all(packed, ('py', 'pz'), split_axis=0, concat_axis=0, tiled=T...]
    dot_general x0 -> x1, local copies, waits for them, and re-layouts: none -> 5.54 us  [shards(): cells = jnp.einsum('ypz,zk->ypk', source, depth_basis, precision=HIGH)]
    div x0 -> x1, other arithmetic: none -> 5.06 us  [shards(): (modes[:, :planes] + c1 * local_basis[0][:, None, None] * below + c1 * lo...]
    dot_general x9 -> x8, matrix products: 37.4 us -> 40.1 us  [the longest x1 10.4 us: shards(): modes = jnp.einsum('mpk,pi->mik', cells, forward, precision=HIGH)]
    pallas_call x0 -> x1, Pallas kernels: none -> 2.67 us  [shards(): pl.pallas_call(functools.partial(chain_kernel, planes), out_shape=(jax.Sh...]
  transfers between devices with their start and end apart: 2 -> 2, of which waited for: 1 -> 2; matrix products, arithmetic and copies ran while one was open for 5% -> 6% of each run, Pallas kernels for 0% -> 0%
where the time goes in v2:
time: 136 us; the launch traced here: 135 us
  matrix products  58.7 us (43%)
  other arithmetic  23.4 us (17%)
  waiting for transfers between devices  14.8 us (11%)
  local copies, waits for them, and re-layouts  12.5 us (9%)
  starting transfers between devices  10 us (7%)
  blocking collectives  9.98 us (7%)
  between operations  3.15 us (2%)
  Pallas kernels  2.67 us (2%)
    all_to_all x2, waiting for transfers between devices, shards(): lax.all_to_all(packed, ('py', 'pz'), split_axis=0, concat_axis=0, tiled=T...  14.8 us
    dot_general x1, matrix products, shards(): modes = jnp.einsum('mpk,pi->mik', cells, forward, precision=HIGH)  10.4 us
    all_to_all x2, starting transfers between devices, shards(): lax.all_to_all(packed, ('py', 'pz'), split_axis=0, concat_axis=0, tiled=T...  10 us
    all_gather x1, blocking collectives, shards(): lax.all_gather(jnp.concatenate([moments, shared], axis=0), 'blk', axis=0)  9.98 us
    dot_general x1, matrix products, shards(): ends = jnp.einsum('mik,iq->mqk', slab, pick, precision=HIGHEST)  6.77 us
    dot_general x1, matrix products, shards(): jnp.einsum('kji,iq->qkj', joined / spectra, pick, precision=HIGHEST)  6.48 us
    dot_general x1, matrix products, shards(): jnp.einsum('kji,dsj->dksi', total, beside_basis, precision=HIGHEST)  6.07 us
    dot_general x1, matrix products, shards(): jnp.einsum('rki,rj->kji', seams, seam_basis, precision=HIGHEST)  5.66 us
  transfers between devices with their start and end apart: 2, of which 2 were waited for; matrix products, arithmetic and copies ran while one was open for 6% of the time, Pallas kernels for 0%

profile of v2, /device:TPU:0, one launch (start us, length us, event | category | flops | bytes accessed | tf_op | source)
XLA Modules:
  0.0 135.1 jit_solution(8705979078894142180)
XLA Ops:
  0.7 4.0 %multiply_reduce_fusion.2 = f32[]{:T(128)} fusion(f32[32,256,128]{2,1,0:T(8,128)} %param.20), kind=kLoop, calls=%fused_computation.26 | loop fusion | flops 2097151 | bytes 4194308 | tf_op jit(solution)/shard_map/reduce_sum | solution.py:176
  4.7 0.6 fusion.67
  5.3 4.9 %convolution_bitcast_fusion = f32[32,256,128]{1,2,0:T(8,128)} fusion(f32[128,128,1]{0,1,2:T(8,128)} %constant.102, f32[32,256,128]{2,1,0:T(8,128)S(1)} %copy-done), kind=kOutput, calls=%fused_computation.30 | convolution fusion | flops 805306368 | bytes 8454144 | tf_op jit(solution)/shard_map/ypz,zk->ypk/dot_general | solution.py:161
  10.2 0.0 copy-start.15
  10.2 0.0 copy-start.5
  10.2 5.5 %copy.67 = f32[32,256,128]{2,0,1:T(8,128)} copy(f32[32,256,128]{1,2,0:T(8,128)} %convolution_bitcast_fusion) | data formatting | bytes 8388608 | tf_op jit(solution)/shard_map/ypz,zk->ypk/dot_general | solution.py:161
  15.8 0.6 fusion.61
  17.1 0.6 broadcast_multiply_fusion.3
  17.7 0.7 broadcast_multiply_fusion
  18.4 0.6 broadcast_multiply_fusion.4
  18.9 0.1 broadcast_add_fusion.3
  19.0 4.2 %fusion.68 = f32[32,256,128]{2,0,1:T(8,128)S(1)} fusion(f32[32,32,1]{0,1,2:T(8,128)S(1)} %copy-done.5, f32[32,256,128]{2,0,1:T(8,128)} %copy.67), kind=kOutput, calls=%fused_computation.104 | convolution fusion | flops 201326592 | bytes 8392704 | tf_op jit(solution)/shard_map/ypk,ym->mpk/dot_general | solution.py:162
  23.3 10.4 %multiply_reduce_fusion.1 = (f32[384,128]{1,0:T(8,128)S(1)}, f32[384,128]{1,0:T(8,128)S(1)}, f32[32,384,128]{2,1,0:T(8,128)}, f32[32,384,128]{2,1,0:T(8,128)}) fusion(f32[32]{0:T(128)S(1)} %copy-done.21, f32[128]{0:T(128)S(1)} %broadcast_multiply_fusion.3, f32[32,384]{1,0:T(8,128)S(1)} %broadcast_add_fusion.3, f32[32]{0:T(128)S(1)} %copy-done.14, ...), kind=kOutput, calls=%fused_computation.3 | convolution fusion | flops 2425356288 | bytes 18006784 | tf_op jit(solution)/shard_map/mpk,pi->mik/dot_general | solution.py:163
  33.8 0.1 copy.69
  33.9 0.1 copy.70
  34.0 0.9 slice.118
  35.0 6.8 %fusion.34 = f32[32,4,128]{2,1,0:T(4,128)S(1)} fusion(f32[32,2,128]{2,1,0:T(2,128)S(1)} %slice.118, f32[384,4]{0,1:T(4,128)S(1)} %copy-done.23, f32[384,4]{0,1:T(4,128)S(1)} %copy-done.22, f32[]{:T(128)} %bitcast.9, f32[32,384,128]{2,1,0:T(8,128)} %get-tuple-element.23, f32[128]{0:T(128)S(1)} %broadcast_multiply_fusion.3, f32[32,384]{1,0:T(8,128)S(1)} %broadcast_add_fusion.3), kind=kOutput, calls=%fused_computation.41 | convolution fusion | flops 78662656 | bytes 6451716 | tf_op jit(solution)/shard_map/mik,iq->mqk/dot_general | solution.py:172
  41.8 0.2 convolution_bitcast_fusion.2
  42.0 0.1 copy.73
  42.2 0.2 concatenate.45
  42.4 0.7 pad.17.clone
  43.0 0.8 pad_maximum_fusion
  43.8 6.4 %all-to-all-start = ((f32[8,16,896]{2,1,0:T(8,128)}), f32[8,16,896]{2,1,0:T(8,128)S(1)}, u32[]{:S(2)}, u32[]{:S(2)}) async-start(f32[8,16,896]{2,1,0:T(8,128)} %pad_maximum_fusion), calls=%async_computation | async-start | bytes 917504 | tf_op jit(solution)/shard_map/all_to_all | solution.py:187
  51.5 0.7 dynamic-slice_multiply_fusion
  52.2 0.6 copy.79.ids_ref
  52.8 0.6 gather_fusion
  53.4 0.6 broadcast_multiply_fusion.1
  54.0 1.4 %broadcast_add_fusion.4 = (f32[16,256]{1,0:T(8,128)S(1)}, f32[16,256]{1,0:T(8,128)}, f32[16,256]{1,0:T(8,128)}) fusion(f32[16]{0:T(128)S(1)} %dynamic-slice_multiply_fusion, f32[256]{0:T(256)S(1)} %broadcast_multiply_fusion.1, f32[]{:T(128)} %bitcast.9), kind=kLoop, calls=%fused_computation.78 | loop fusion | flops 40960 | bytes 50244 | tf_op jit(solution)/shard_map/add | solution.py:203
  55.3 2.9 %broadcast_add_fusion = f32[16,256,384]{2,1,0:T(8,128)} fusion(f32[16,256]{1,0:T(8,128)S(1)} %get-tuple-element.17, f32[384]{0:T(512)S(1)} %broadcast_multiply_fusion), kind=kLoop, calls=%fused_computation.27 | loop fusion | flops 1572864 | bytes 6309376 | tf_op jit(solution)/shard_map/add | solution.py:204
  58.3 5.9 %all-to-all-done = f32[8,16,896]{2,1,0:T(8,128)S(1)} async-done(((f32[8,16,896]{2,1,0:T(8,128)}), f32[8,16,896]{2,1,0:T(8,128)S(1)}, u32[]{:S(2)}, u32[]{:S(2)}) %all-to-all-start) | async-done | bytes 458784 | tf_op jit(solution)/shard_map/all_to_all | solution.py:187
  64.1 0.1 copy.98
  64.2 0.1 copy.99
  64.4 0.2 reshape.136
  64.5 0.4 convolution_bitcast_fusion.4
  65.0 5.7 %multiply_bitcast_fusion = f32[16,256,384]{2,1,0:T(8,128)S(1)} fusion(f32[]{:T(128)} %bitcast.7, f32[1,16,384]{2,0,1:T(1,128)S(1)} %broadcast_in_dim.36, f32[7,16,384]{2,0,1:T(8,128)S(1)} %copy.99, f32[7,16,384]{2,0,1:T(8,128)S(1)} %copy.98, f32[8,256]{1,0:T(8,128)S(1)} %copy-done.7, f32[8,256]{1,0:T(8,128)S(1)} %gather_fusion), kind=kOutput, calls=%fused_computation.1 | convolution fusion | flops 303861760 | bytes 6676484 | tf_op jit(solution)/shard_map/rki,rj->kji/dot_general | solution.py:201
  70.7 6.5 %fusion.35 = f32[4,16,256]{2,0,1:T(4,128)S(1)} fusion(f32[16,256,384]{2,1,0:T(8,128)S(1)} %multiply_bitcast_fusion, f32[16,256]{1,0:T(8,128)S(1)} %get-tuple-element.17, f32[384]{0:T(512)S(1)} %broadcast_multiply_fusion, f32[16,4,256]{2,0,1:T(8,128)S(1)} %convolution_bitcast_fusion.4, f32[384,4]{0,1:T(4,128)S(1)} %copy-done.23, ...), kind=kOutput, calls=%fused_computation.43 | convolution fusion | flops 78662656 | bytes 6452740 | tf_op jit(solution)/shard_map/kji,iq->qkj/dot_general | solution.py:205
  77.2 0.7 slice_reduce_fusion
  77.9 0.7 concatenate.48.clone
  78.5 10.0 %all-gather = f32[20,16,256]{2,1,0:T(8,128)} all-gather(f32[5,16,256]{2,1,0:T(8,128)S(1)} %concatenate.48.clone), channel_id=2, replica_groups=mesh['blk'=4,'py'=4,'pz'=2] {'blk'}, dimensions={0}, use_global_device_ids=true | all-gather | bytes 409600 | tf_op jit(solution)/shard_map/all_gather | solution.py:210
  88.5 2.7 %chain.1 = (f32[2,16,256]{2,1,0:T(8,128)}, f32[2,16,256]{2,1,0:T(8,128)}) custom-call(s32[4,2]{1,0:T(4,128)} %copy.79.ids_ref, s32[1]{0:T(128)} %bitcast.20.own_ref, f32[1]{0:T(128)} %get-tuple-element.20.c0_ref, f32[16,256]{1,0:T(8,128)} %get-tuple-element.18.theta_ref, f32[16,256]{1,0:T(8,128)} %get-tuple-element.19.sinh_ref, f32[4,5,16,256]{3,2,1,0:T(8,128)} %bitcast.108), custom_call_target="tpu_custom_call" | custom-call | tf_op jit(solution)/shard_map/chain/pallas_call | solution.py:218
  91.2 0.7 slice_bitcast_fusion.3
  91.9 1.5 %convolution_bitcast_fusion.1 = f32[8,16,2,32]{3,1,0,2:T(8,128)S(1)} fusion(f32[8,32,256,1]{2,1,0,3:T(8,128)S(1)} %copy-done.2, f32[2,16,256]{2,1,0:T(8,128)} %get-tuple-element.4), kind=kOutput, calls=%fused_computation.38 | convolution fusion | flops 25165824 | bytes 327680 | tf_op jit(solution)/shard_map/skj,dyj->dksy/dot_general | solution.py:238
  93.4 0.9 reduce_sum.77
  94.3 0.1 pad.8.clone
  94.3 6.1 %fusion.31 = f32[8,16,2,256]{3,0,1,2:T(8,128)S(1)} fusion(f32[8,2,256,1]{2,0,3,1:T(8,128)S(1)} %copy-done.20, f32[16,256,384]{2,1,0:T(8,128)} %broadcast_add_fusion, f32[16,256,384]{2,1,0:T(8,128)} %copy-done.1, f32[256]{0:T(256)S(1)} %copy-done.10, f32[16,256]{1,0:T(8,128)S(1)} %get-tuple-element.16, f32[256]{0:T(256)S(1)} %copy-done.11, ...), kind=kOutput, calls=%fused_computation.37 | convolution fusion | flops 206700544 | bytes 9095168 | tf_op jit(solution)/shard_map/kji,dsj->dksi/dot_general | solution.py:236
  100.4 0.2 copy.80
  100.6 0.2 concatenate.51
  100.9 0.1 copy.81
  101.0 0.1 concatenate.52
  101.1 0.7 maximum_maximum_fusion
  101.9 3.7 %all-to-all-start.1 = ((f32[8,16,578]{2,1,0:T(8,128)}), f32[8,16,578]{2,1,0:T(8,128)S(1)}, u32[]{:S(2)}, u32[]{:S(2)}) async-start(f32[8,16,578]{2,1,0:T(8,128)} %maximum_maximum_fusion), calls=%async_computation.1 | async-start | bytes 655360 | tf_op jit(solution)/shard_map/all_to_all | solution.py:249
  105.5 0.6 broadcast_multiply_fusion.6
  106.1 1.3 slice_reduce_fusion.1
  107.4 8.9 %all-to-all-done.1 = f32[8,16,578]{2,1,0:T(8,128)S(1)} async-done(((f32[8,16,578]{2,1,0:T(8,128)}), f32[8,16,578]{2,1,0:T(8,128)S(1)}, u32[]{:S(2)}, u32[]{:S(2)}) %all-to-all-start.1) | async-done | bytes 295968 | tf_op jit(solution)/shard_map/all_to_all | solution.py:249
  116.4 0.1 slice.113
  116.5 0.1 copy.84
  116.5 0.2 convolution_bitcast_fusion.5
  116.7 0.1 copy.82
  116.8 0.1 copy.83
  116.9 5.1 %slice_divide_fusion = f32[32,256,128]{2,1,0:T(8,128)S(1)} fusion(f32[32,384,128]{2,1,0:T(8,128)} %get-tuple-element.12, f32[32,384,128]{2,1,0:T(8,128)} %get-tuple-element.23, f32[32,128]{1,0:T(8,128)S(1)} %get-tuple-element.14, f32[256]{0:T(256)S(1)} %copy-done.10, f32[32,128]{1,0:T(8,128)S(1)} %get-tuple-element.13, f32[256]{0:T(256)S(1)} %copy-done.11, ...), kind=kLoop, calls=%fused_computation.6 | loop fusion | flops 9437184 | bytes 12880128 | tf_op jit(solution)/shard_map/div | solution.py:261
  122.0 4.2 %fusion.14 = f32[32,256,128]{2,0,1:T(8,128)S(1)} fusion(f32[32,32,1]{0,1,2:T(8,128)S(1)} %copy-done.5, f32[32,256,128]{2,1,0:T(8,128)S(1)} %slice_divide_fusion), kind=kOutput, calls=%fused_computation.20 | convolution fusion | flops 201326592 | bytes 8392704 | tf_op jit(solution)/shard_map/mik,ym->yik/dot_general | solution.py:268
  126.3 4.3 %fusion.12 = f32[256,32,128]{2,0,1:T(8,128)S(1)} fusion(f32[32,256,128]{2,0,1:T(8,128)S(1)} %fusion.14, f32[256,256]{1,0:T(8,128)S(1)} %copy-done.6, f32[256,256]{1,0:T(8,128)S(1)} %copy-done.3, pred[]{:T(512)S(6)} %eq.11), kind=kOutput, calls=%fused_computation.18 | convolution fusion | flops 1610678272 | bytes 8912897 | tf_op jit(solution)/shard_map/yik,pi->ypk/dot_general | solution.py:269
  130.6 3.3 %fusion.10 = f32[32,256,128]{2,1,0:T(8,128)} fusion(f32[128,128,1]{0,1,2:T(8,128)S(1)} %copy-done.4, f32[256,32,128]{2,0,1:T(8,128)S(1)} %fusion.12), kind=kOutput, calls=%fused_computation.16 | convolution fusion | flops 805306368 | bytes 8454144 | tf_op jit(solution)/shard_map/ypk,zk->ypz/dot_general | solution.py:270
  133.9 1.2 fusion.62
  (59 shorter events, 0.3 us)
Async XLA Ops:
  0.6 4.1 %copy-start.8 = (f32[3]{0:T(128)S(1)}, f32[3]{0:T(128)}, u32[]{:S(2)}) copy-start(f32[3]{0:T(128)} %param.21) | copy-start | bytes 40
  0.6 4.7 %copy-start = (f32[32,256,128]{2,1,0:T(8,128)S(1)}, f32[32,256,128]{2,1,0:T(8,128)}, u32[]{:S(2)}) copy-start(f32[32,256,128]{2,1,0:T(8,128)} %param.20) | copy-start | bytes 12582916
  10.2 5.6 %copy-start.17 = (s32[4]{0:T(128)S(1)}, s32[4]{0:T(128)}, u32[]{:S(2)}) copy-start(s32[4]{0:T(128)} %param.23) | copy-start | bytes 52
  10.2 6.9 %copy-start.16 = (f32[128]{0:T(128)S(1)}, f32[128]{0:T(128)}, u32[]{:S(2)}) copy-start(f32[128]{0:T(128)} %constant.72.clone) | copy-start | bytes 1540
  10.2 7.5 %copy-start.9 = (f32[384]{0:T(512)S(1)}, f32[384]{0:T(512)}, u32[]{:S(2)}) copy-start(f32[384]{0:T(512)} %constant.73.clone) | copy-start | bytes 4612
  10.2 8.2 %copy-start.14 = (f32[32]{0:T(128)S(1)}, f32[32]{0:T(128)}, u32[]{:S(2)}) copy-start(f32[32]{0:T(128)} %constant.95) | copy-start | bytes 388
  10.2 8.2 %copy-start.15 = (f32[32]{0:T(128)S(1)}, f32[32]{0:T(128)}, u32[]{:S(2)}) copy-start(f32[32]{0:T(128)} %constant.71.clone) | copy-start | bytes 388
  10.2 8.8 %copy-start.5 = (f32[32,32,1]{0,1,2:T(8,128)S(1)}, f32[32,32,1]{0,1,2:T(8,128)}, u32[]{:S(2)}) copy-start(f32[32,32,1]{0,1,2:T(8,128)} %constant.101) | copy-start | bytes 12292
  19.0 4.2 %copy-start.18 = (f32[256,384]{0,1:T(8,128)S(1)}, f32[256,384]{0,1:T(8,128)}, u32[]{:S(2)}) copy-start(f32[256,384]{0,1:T(8,128)} %constant.89) | copy-start | bytes 1179652
  19.0 4.2 %copy-start.19 = (f32[256,384]{0,1:T(8,128)S(1)}, f32[256,384]{0,1:T(8,128)}, u32[]{:S(2)}) copy-start(f32[256,384]{0,1:T(8,128)} %constant.74.clone) | copy-start | bytes 1179652
  19.0 4.2 %copy-start.21 = (f32[32]{0:T(128)S(1)}, f32[32]{0:T(128)}, u32[]{:S(2)}) copy-start(f32[32]{0:T(128)} %constant.91) | copy-start | bytes 388
  23.3 11.7 %copy-start.22 = (f32[384,4]{0,1:T(4,128)S(1)}, f32[384,4]{0,1:T(4,128)}, u32[]{:S(2)}) copy-start(f32[384,4]{0,1:T(4,128)} %constant.76.clone) | copy-start | bytes 18436
  23.3 11.7 %copy-start.23 = (f32[384,4]{0,1:T(4,128)S(1)}, f32[384,4]{0,1:T(4,128)}, u32[]{:S(2)}) copy-start(f32[384,4]{0,1:T(4,128)} %constant.75.clone) | copy-start | bytes 18436
  35.0 17.2 %copy-start.12 = (s32[4,2]{0,1:T(2,128)S(1)}, s32[4,2]{0,1:T(2,128)}, u32[]{:S(2)}) copy-start(s32[4,2]{0,1:T(2,128)} %param.22) | copy-start | bytes 100
  35.0 17.9 %copy-start.3 = (f32[256,256]{1,0:T(8,128)S(1)}, f32[256,256]{1,0:T(8,128)}, u32[]{:S(2)}) copy-start(f32[256,256]{1,0:T(8,128)} %constant.66.clone) | copy-start | bytes 786436
  35.0 18.4 %copy-start.13 = (f32[256]{0:T(256)S(1)}, f32[256]{0:T(256)}, u32[]{:S(2)}) copy-start(f32[256]{0:T(256)} %constant.70.clone) | copy-start | bytes 3076
  43.8 20.3 %all-to-all-start = ((f32[8,16,896]{2,1,0:T(8,128)}), f32[8,16,896]{2,1,0:T(8,128)S(1)}, u32[]{:S(2)}, u32[]{:S(2)}) async-start(f32[8,16,896]{2,1,0:T(8,128)} %pad_maximum_fusion), calls=%async_computation | async-start | bytes 917504 | tf_op jit(solution)/shard_map/all_to_all | solution.py:187
  55.3 9.2 %copy-start.2 = (f32[8,32,256,1]{2,1,0,3:T(8,128)S(1)}, f32[8,32,256,1]{2,1,0,3:T(8,128)}, u32[]{:S(2)}) copy-start(f32[8,32,256,1]{2,1,0,3:T(8,128)} %constant.103) | copy-start | bytes 786436
  55.3 9.6 %copy-start.7 = (f32[8,256]{1,0:T(8,128)S(1)}, f32[8,256]{1,0:T(8,128)}, u32[]{:S(2)}) copy-start(f32[8,256]{1,0:T(8,128)} %constant.93) | copy-start | bytes 24580
  70.6 6.5 %copy-start.1 = (f32[16,256,384]{2,1,0:T(8,128)}, f32[16,256,384]{2,1,0:T(8,128)S(1)}, u32[]{:S(2)}) copy-start(f32[16,256,384]{2,1,0:T(8,128)S(1)} %multiply_bitcast_fusion) | copy-start | bytes 18874372
  70.7 23.7 %copy-start.10 = (f32[256]{0:T(256)S(1)}, f32[256]{0:T(256)}, u32[]{:S(2)}) copy-start(f32[256]{0:T(256)} %constant.100) | copy-start | bytes 3076
  70.7 23.7 %copy-start.11 = (f32[256]{0:T(256)S(1)}, f32[256]{0:T(256)}, u32[]{:S(2)}) copy-start(f32[256]{0:T(256)} %constant.98) | copy-start | bytes 3076
  70.7 23.7 %copy-start.20 = (f32[8,2,256,1]{2,0,3,1:T(8,128)S(1)}, f32[8,2,256,1]{2,0,3,1:T(8,128)}, u32[]{:S(2)}) copy-start(f32[8,2,256,1]{2,0,3,1:T(8,128)} %constant.104) | copy-start | bytes 49156
  101.9 14.5 %all-to-all-start.1 = ((f32[8,16,578]{2,1,0:T(8,128)}), f32[8,16,578]{2,1,0:T(8,128)S(1)}, u32[]{:S(2)}, u32[]{:S(2)}) async-start(f32[8,16,578]{2,1,0:T(8,128)} %maximum_maximum_fusion), calls=%async_computation.1 | async-start | bytes 655360 | tf_op jit(solution)/shard_map/all_to_all | solution.py:249
  122.0 4.3 %copy-start.6 = (f32[256,256]{1,0:T(8,128)S(1)}, f32[256,256]{1,0:T(8,128)}, u32[]{:S(2)}) copy-start(f32[256,256]{1,0:T(8,128)} %constant.88) | copy-start | bytes 786436
  126.3 4.3 %copy-start.4 = (f32[128,128,1]{0,1,2:T(8,128)S(1)}, f32[128,128,1]{0,1,2:T(8,128)}, u32[]{:S(2)}) copy-start(f32[128,128,1]{0,1,2:T(8,128)} %constant.102) | copy-start | bytes 196612

commit v3 on v2

--- a/solution.py
+++ b/solution.py
@@ -158,8 +158,8 @@
     backward = jnp.where(flipped, own_table[::-1], own_table)
     pick = jnp.asarray(box_pick) + c0 * jnp.asarray(margin_pick)
 
-    cells = jnp.einsum("ypz,zk->ypk", source, depth_basis, precision=HIGH)
-    cells = jnp.einsum("ypk,ym->mpk", cells, local_basis, precision=HIGH)
+    cells = jnp.einsum("ypz,ym->mpz", source, local_basis, precision=HIGH)
+    cells = jnp.einsum("mpz,zk->mpk", cells, depth_basis, precision=HIGH)
     modes = jnp.einsum("mpk,pi->mik", cells, forward, precision=HIGH)
     slab_spectra = (
         c0 * mu_plane[None, :, None]
@@ -169,7 +169,7 @@
     slab = modes / slab_spectra
     edge_first = jnp.sum(slab * local_basis[0][:, None, None], axis=0)
     edge_last = jnp.sum(slab * local_basis[-1][:, None, None], axis=0)
-    ends = jnp.einsum("mik,iq->mqk", slab, pick, precision=HIGHEST)
+    ends = jnp.einsum("mik,iq->mqk", slab, pick, precision=HIGH)
     plain = jnp.zeros((rows, 2, depth), jnp.float32)
     ends = ends + jnp.concatenate([plain, modes[:, count - 2 :]], axis=1)
     ends = jnp.einsum("mqk,ym->kqy", ends, local_basis, precision=HIGHEST)
@@ -198,11 +198,11 @@
     last_rows = row_basis[rows * np.arange(group) + rows - 1]
     seam_basis = jnp.concatenate([first_rows, last_rows], axis=0)
     seams = jnp.concatenate([below, above], axis=0)
-    joined = c1 * jnp.einsum("rki,rj->kji", seams, seam_basis, precision=HIGHEST)
+    joined = c1 * jnp.einsum("rki,rj->kji", seams, seam_basis, precision=HIGH)
     held_depth = lax.dynamic_slice_in_dim(mu_depth, member * own_depth, own_depth)
     cross = c1 * mu_row[None, :] + c2 * held_depth[:, None]
     spectra = c0 * mu_plane[None, None, :] + cross[:, :, None]
-    moments = jnp.einsum("kji,iq->qkj", joined / spectra, pick, precision=HIGHEST)
+    moments = jnp.einsum("kji,iq->qkj", joined / spectra, pick, precision=HIGH)
     moments = moments + jnp.einsum(
         "dkqy,dyj->qkj", ends, row_basis.reshape(group, rows, all_rows), precision=HIGHEST
     )
@@ -233,7 +233,7 @@
         + pushes[1][:, :, None] * last_col
     )
     total = total / spectra[:, :, :planes]
-    beside_values = jnp.einsum("kji,dsj->dksi", total, beside_basis, precision=HIGHEST)
+    beside_values = jnp.einsum("kji,dsj->dksi", total, beside_basis, precision=HIGH)
     beside_values = beside_values + jnp.stack([below, above], axis=2)[:, :, :, :planes]
     pushes = jnp.einsum(
         "skj,dyj->dksy", pushes, row_basis.reshape(group, rows, all_rows), precision=HIGHEST

time: 136 us -> 124 us (0.912)
  matrix products: 58.7 us -> 52.1 us
  local copies, waits for them, and re-layouts: 12.5 us -> 6.96 us
    dot_general x1 -> x0, local copies, waits for them, and re-layouts: 5.54 us -> none  [shards(): cells = jnp.einsum('ypz,zk->ypk', source, depth_basis, precision=HIGH)]
    dot_general x6, matrix products: 34.1 us -> 30.7 us  [the longest x1 6.31 us: shards(): cells = jnp.einsum('mpz,zk->mpk', cells, depth_basis, precision=HIGH)]
    dot_general x1, matrix products: 10.4 us -> 7.19 us  [shards(): modes = jnp.einsum('mpk,pi->mik', cells, forward, precision=HIGH)]
  transfers between devices with their start and end apart: 2 -> 2, of which waited for: 2 -> 2; matrix products, arithmetic and copies ran while one was open for 6% -> 7% of each run, Pallas kernels for 0% -> 0%
where the time goes in v3:
time: 124 us; the launch traced here: 123 us
  matrix products  52.1 us (42%)
  other arithmetic  23.4 us (19%)
  waiting for transfers between devices  14.8 us (12%)
  starting transfers between devices  10 us (8%)
  blocking collectives  9.96 us (8%)
  local copies, waits for them, and re-layouts  6.96 us (6%)
  between operations  3.08 us (2%)
  Pallas kernels  2.67 us (2%)
    all_to_all x2, waiting for transfers between devices, shards(): lax.all_to_all(packed, ('py', 'pz'), split_axis=0, concat_axis=0, tiled=T...  14.8 us
    all_to_all x2, starting transfers between devices, shards(): lax.all_to_all(packed, ('py', 'pz'), split_axis=0, concat_axis=0, tiled=T...  10 us
    all_gather x1, blocking collectives, shards(): lax.all_gather(jnp.concatenate([moments, shared], axis=0), 'blk', axis=0)  9.96 us
    dot_general x1, matrix products, shards(): modes = jnp.einsum('mpk,pi->mik', cells, forward, precision=HIGH)  7.19 us
    dot_general x1, matrix products, shards(): cells = jnp.einsum('mpz,zk->mpk', cells, depth_basis, precision=HIGH)  6.31 us
    dot_general x1, matrix products, shards(): cells = jnp.einsum('ypz,ym->mpz', source, local_basis, precision=HIGH)  6.16 us
    dot_general x1, matrix products, shards(): ends = jnp.einsum('mik,iq->mqk', slab, pick, precision=HIGH)  5.93 us
    dot_general x1, matrix products, shards(): jnp.einsum('kji,dsj->dksi', total, beside_basis, precision=HIGH)  5.24 us
  transfers between devices with their start and end apart: 2, of which 2 were waited for; matrix products, arithmetic and copies ran while one was open for 7% of the time, Pallas kernels for 0%

profile of v3, /device:TPU:0, one launch (start us, length us, event | category | flops | bytes accessed | tf_op | source)
XLA Modules:
  0.0 122.9 jit_solution(13255882989000739995)
XLA Ops:
  0.6 0.0 copy-start.5
  0.7 4.0 %multiply_reduce_fusion.2 = f32[]{:T(128)} fusion(f32[32,256,128]{2,1,0:T(8,128)} %param.20), kind=kLoop, calls=%fused_computation.28 | loop fusion | flops 2097151 | bytes 4194308 | tf_op jit(solution)/shard_map/reduce_sum | solution.py:176
  4.7 0.6 fusion.66
  5.3 0.0 copy-start.9
  5.3 0.0 copy-start.14
  5.4 6.2 %fusion.18 = f32[32,256,128]{2,0,1:T(8,128)} fusion(f32[32,32,1]{0,1,2:T(8,128)S(1)} %copy-done.5, f32[32,256,128]{2,1,0:T(8,128)S(1)} %copy-done), kind=kOutput, calls=%fused_computation.24 | convolution fusion | flops 201326592 | bytes 8392704 | tf_op jit(solution)/shard_map/ypz,ym->mpz/dot_general | solution.py:161
  11.5 0.6 fusion.60
  12.8 0.6 broadcast_multiply_fusion.3
  13.4 0.7 broadcast_multiply_fusion
  14.1 0.6 broadcast_multiply_fusion.4
  14.6 0.1 broadcast_add_fusion.3
  14.7 6.3 %fusion.16 = f32[32,256,128]{2,1,0:T(8,128)S(1)} fusion(f32[128,128,1]{1,0,2:T(8,128)S(1)} %copy-done.4, f32[32,256,128]{2,0,1:T(8,128)} %fusion.18), kind=kOutput, calls=%fused_computation.22 | convolution fusion | flops 805306368 | bytes 8454144 | tf_op jit(solution)/shard_map/mpz,zk->mpk/dot_general | solution.py:162
  21.1 7.2 %multiply_reduce_fusion.1 = (f32[384,128]{1,0:T(8,128)S(1)}, f32[384,128]{1,0:T(8,128)S(1)}, f32[32,384,128]{2,1,0:T(8,128)}, f32[32,384,128]{2,1,0:T(8,128)}) fusion(f32[32]{0:T(128)S(1)} %copy-done.21, f32[128]{0:T(128)S(1)} %broadcast_multiply_fusion.3, f32[32,384]{1,0:T(8,128)S(1)} %broadcast_add_fusion.3, f32[32]{0:T(128)S(1)} %copy-done.14, ...), kind=kOutput, calls=%fused_computation.3 | convolution fusion | flops 2425356288 | bytes 18006784 | tf_op jit(solution)/shard_map/mpk,pi->mik/dot_general | solution.py:163
  28.3 0.1 copy.68
  28.4 0.1 copy.69
  28.6 0.9 slice.118
  29.6 5.9 %fusion.33 = f32[32,4,128]{2,1,0:T(4,128)S(1)} fusion(f32[32,2,128]{2,1,0:T(2,128)S(1)} %slice.118, f32[384,4]{0,1:T(4,128)S(1)} %copy-done.23, f32[384,4]{0,1:T(4,128)S(1)} %copy-done.22, f32[]{:T(128)} %bitcast.8, f32[32,384,128]{2,1,0:T(8,128)} %get-tuple-element.23, f32[128]{0:T(128)S(1)} %broadcast_multiply_fusion.3, f32[32,384]{1,0:T(8,128)S(1)} %broadcast_add_fusion.3), kind=kOutput, calls=%fused_computation.42 | convolution fusion | flops 40913920 | bytes 6451716 | tf_op jit(solution)/shard_map/mik,iq->mqk/dot_general | solution.py:172
  35.5 0.2 convolution_bitcast_fusion.2
  35.8 0.1 copy.72
  35.9 0.2 concatenate.45
  36.1 0.7 pad.17.clone
  36.8 0.8 pad_maximum_fusion
  37.6 6.4 %all-to-all-start = ((f32[8,16,896]{2,1,0:T(8,128)}), f32[8,16,896]{2,1,0:T(8,128)S(1)}, u32[]{:S(2)}, u32[]{:S(2)}) async-start(f32[8,16,896]{2,1,0:T(8,128)} %pad_maximum_fusion), calls=%async_computation | async-start | bytes 917504 | tf_op jit(solution)/shard_map/all_to_all | solution.py:187
  45.2 0.7 dynamic-slice_multiply_fusion
  45.9 0.6 copy.78.ids_ref
  46.6 0.6 gather_fusion
  47.1 0.6 broadcast_multiply_fusion.1
  47.7 1.4 %broadcast_add_fusion.4 = (f32[16,256]{1,0:T(8,128)S(1)}, f32[16,256]{1,0:T(8,128)}, f32[16,256]{1,0:T(8,128)}) fusion(f32[16]{0:T(128)S(1)} %dynamic-slice_multiply_fusion, f32[256]{0:T(256)S(1)} %broadcast_multiply_fusion.1, f32[]{:T(128)} %bitcast.8), kind=kLoop, calls=%fused_computation.79 | loop fusion | flops 40960 | bytes 50244 | tf_op jit(solution)/shard_map/add | solution.py:203
  49.1 2.9 %broadcast_add_fusion = f32[16,256,384]{2,1,0:T(8,128)} fusion(f32[16,256]{1,0:T(8,128)S(1)} %get-tuple-element.17, f32[384]{0:T(512)S(1)} %broadcast_multiply_fusion), kind=kLoop, calls=%fused_computation.29 | loop fusion | flops 1572864 | bytes 6309376 | tf_op jit(solution)/shard_map/add | solution.py:204
  52.0 5.9 %all-to-all-done = f32[8,16,896]{2,1,0:T(8,128)S(1)} async-done(((f32[8,16,896]{2,1,0:T(8,128)}), f32[8,16,896]{2,1,0:T(8,128)S(1)}, u32[]{:S(2)}, u32[]{:S(2)}) %all-to-all-start) | async-done | bytes 458784 | tf_op jit(solution)/shard_map/all_to_all | solution.py:187
  57.9 0.1 copy.94
  57.9 0.1 copy.95
  58.1 0.2 reshape.136
  58.3 0.4 convolution_bitcast_fusion.4
  58.7 3.2 %multiply_bitcast_fusion = f32[16,256,384]{2,1,0:T(8,128)S(1)} fusion(f32[]{:T(128)} %bitcast.6, f32[1,16,384]{2,0,1:T(1,128)S(1)} %broadcast_in_dim.36, f32[7,16,384]{2,0,1:T(8,128)S(1)} %copy.95, f32[7,16,384]{2,0,1:T(8,128)S(1)} %copy.94, f32[8,256]{1,0:T(8,128)S(1)} %copy-done.7, f32[8,256]{1,0:T(8,128)S(1)} %gather_fusion), kind=kOutput, calls=%fused_computation.1 | convolution fusion | flops 152866816 | bytes 6676484 | tf_op jit(solution)/shard_map/rki,rj->kji/dot_general | solution.py:201
  62.0 3.8 %fusion.34 = f32[4,16,256]{2,0,1:T(4,128)S(1)} fusion(f32[16,256,384]{2,1,0:T(8,128)S(1)} %multiply_bitcast_fusion, f32[16,256]{1,0:T(8,128)S(1)} %get-tuple-element.17, f32[384]{0:T(512)S(1)} %broadcast_multiply_fusion, f32[16,4,256]{2,0,1:T(8,128)S(1)} %convolution_bitcast_fusion.4, f32[384,4]{0,1:T(4,128)S(1)} %copy-done.23, ...), kind=kOutput, calls=%fused_computation.44 | convolution fusion | flops 40913920 | bytes 6452740 | tf_op jit(solution)/shard_map/kji,iq->qkj/dot_general | solution.py:205
  65.8 0.7 slice_reduce_fusion
  66.5 0.7 concatenate.48.clone
  67.2 10.0 %all-gather = f32[20,16,256]{2,1,0:T(8,128)} all-gather(f32[5,16,256]{2,1,0:T(8,128)S(1)} %concatenate.48.clone), channel_id=2, replica_groups=mesh['blk'=4,'py'=4,'pz'=2] {'blk'}, dimensions={0}, use_global_device_ids=true | all-gather | bytes 409600 | tf_op jit(solution)/shard_map/all_gather | solution.py:210
  77.1 2.7 %chain.1 = (f32[2,16,256]{2,1,0:T(8,128)}, f32[2,16,256]{2,1,0:T(8,128)}) custom-call(s32[4,2]{1,0:T(4,128)} %copy.78.ids_ref, s32[1]{0:T(128)} %bitcast.19.own_ref, f32[1]{0:T(128)} %get-tuple-element.20.c0_ref, f32[16,256]{1,0:T(8,128)} %get-tuple-element.18.theta_ref, f32[16,256]{1,0:T(8,128)} %get-tuple-element.19.sinh_ref, f32[4,5,16,256]{3,2,1,0:T(8,128)} %bitcast.104), custom_call_target="tpu_custom_call" | custom-call | tf_op jit(solution)/shard_map/chain/pallas_call | solution.py:218
  79.8 0.7 slice_bitcast_fusion.3
  80.5 1.5 %convolution_bitcast_fusion.1 = f32[8,16,2,32]{3,1,0,2:T(8,128)S(1)} fusion(f32[8,32,256,1]{2,1,0,3:T(8,128)S(1)} %copy-done.2, f32[2,16,256]{2,1,0:T(8,128)} %get-tuple-element.4), kind=kOutput, calls=%fused_computation.39 | convolution fusion | flops 25165824 | bytes 327680 | tf_op jit(solution)/shard_map/skj,dyj->dksy/dot_general | solution.py:238
  82.0 0.9 reduce_sum.77
  82.9 0.1 pad.8.clone
  83.0 5.2 %fusion.30 = f32[8,16,2,256]{3,0,1,2:T(8,128)S(1)} fusion(f32[8,2,256,1]{2,0,3,1:T(8,128)S(1)} %copy-done.20, f32[16,256,384]{2,1,0:T(8,128)} %broadcast_add_fusion, f32[16,256,384]{2,1,0:T(8,128)} %copy-done.1, f32[256]{0:T(256)S(1)} %copy-done.10, f32[16,256]{1,0:T(8,128)S(1)} %get-tuple-element.16, f32[256]{0:T(256)S(1)} %copy-done.11, ...), kind=kOutput, calls=%fused_computation.38 | convolution fusion | flops 106037248 | bytes 9095168 | tf_op jit(solution)/shard_map/kji,dsj->dksi/dot_general | solution.py:236
  88.2 0.2 copy.79
  88.4 0.2 concatenate.51
  88.6 0.1 copy.80
  88.7 0.1 concatenate.52
  88.9 0.7 maximum_maximum_fusion
  89.6 3.7 %all-to-all-start.1 = ((f32[8,16,578]{2,1,0:T(8,128)}), f32[8,16,578]{2,1,0:T(8,128)S(1)}, u32[]{:S(2)}, u32[]{:S(2)}) async-start(f32[8,16,578]{2,1,0:T(8,128)} %maximum_maximum_fusion), calls=%async_computation.1 | async-start | bytes 655360 | tf_op jit(solution)/shard_map/all_to_all | solution.py:249
  93.3 0.6 broadcast_multiply_fusion.6
  93.9 1.3 %slice_reduce_fusion.1 = f32[]{:T(128)} fusion(f32[4,5,16,256]{3,2,1,0:T(8,128)} %bitcast.105), kind=kLoop, calls=%fused_computation.87 | loop fusion | flops 3 | bytes 20 | tf_op jit(solution)/shard_map/reduce_sum | solution.py:273
  95.2 8.9 %all-to-all-done.1 = f32[8,16,578]{2,1,0:T(8,128)S(1)} async-done(((f32[8,16,578]{2,1,0:T(8,128)}), f32[8,16,578]{2,1,0:T(8,128)S(1)}, u32[]{:S(2)}, u32[]{:S(2)}) %all-to-all-start.1) | async-done | bytes 295968 | tf_op jit(solution)/shard_map/all_to_all | solution.py:249
  104.1 0.1 slice.113
  104.2 0.1 copy.83
  104.3 0.2 convolution_bitcast_fusion.5
  104.5 0.1 copy.81
  104.6 0.1 copy.82
  104.7 5.1 %slice_divide_fusion = f32[32,256,128]{2,1,0:T(8,128)S(1)} fusion(f32[32,384,128]{2,1,0:T(8,128)} %get-tuple-element.12, f32[32,384,128]{2,1,0:T(8,128)} %get-tuple-element.23, f32[32,128]{1,0:T(8,128)S(1)} %get-tuple-element.14, f32[256]{0:T(256)S(1)} %copy-done.10, f32[32,128]{1,0:T(8,128)S(1)} %get-tuple-element.13, f32[256]{0:T(256)S(1)} %copy-done.11, ...), kind=kLoop, calls=%fused_computation.6 | loop fusion | flops 9437184 | bytes 12880128 | tf_op jit(solution)/shard_map/div | solution.py:261
  109.8 4.3 %fusion.14 = f32[32,256,128]{2,0,1:T(8,128)S(1)} fusion(f32[32,32,1]{0,1,2:T(8,128)S(1)} %copy-done.5, f32[32,256,128]{2,1,0:T(8,128)S(1)} %slice_divide_fusion), kind=kOutput, calls=%fused_computation.20 | convolution fusion | flops 201326592 | bytes 8392704 | tf_op jit(solution)/shard_map/mik,ym->yik/dot_general | solution.py:268
  114.1 4.3 %fusion.12 = f32[256,32,128]{2,0,1:T(8,128)S(1)} fusion(f32[32,256,128]{2,0,1:T(8,128)S(1)} %fusion.14, f32[256,256]{1,0:T(8,128)S(1)} %copy-done.6, f32[256,256]{1,0:T(8,128)S(1)} %copy-done.3, pred[]{:T(512)S(6)} %eq.11), kind=kOutput, calls=%fused_computation.18 | convolution fusion | flops 1610678272 | bytes 8912897 | tf_op jit(solution)/shard_map/yik,pi->ypk/dot_general | solution.py:269
  118.4 3.3 %fusion.10 = f32[32,256,128]{2,1,0:T(8,128)} fusion(f32[128,128,1]{1,0,2:T(8,128)S(1)} %copy-done.4, f32[256,32,128]{2,0,1:T(8,128)S(1)} %fusion.12), kind=kOutput, calls=%fused_computation.16 | convolution fusion | flops 805306368 | bytes 8454144 | tf_op jit(solution)/shard_map/ypk,zk->ypz/dot_general | solution.py:270
  121.7 1.2 fusion.61
  (58 shorter events, 0.3 us)
Async XLA Ops:
  0.6 4.7 %copy-start.5 = (f32[32,32,1]{0,1,2:T(8,128)S(1)}, f32[32,32,1]{0,1,2:T(8,128)}, u32[]{:S(2)}) copy-start(f32[32,32,1]{0,1,2:T(8,128)} %constant.101) | copy-start | bytes 12292
  0.6 4.1 %copy-start.8 = (f32[3]{0:T(128)S(1)}, f32[3]{0:T(128)}, u32[]{:S(2)}) copy-start(f32[3]{0:T(128)} %param.21) | copy-start | bytes 40
  0.7 4.7 %copy-start = (f32[32,256,128]{2,1,0:T(8,128)S(1)}, f32[32,256,128]{2,1,0:T(8,128)}, u32[]{:S(2)}) copy-start(f32[32,256,128]{2,1,0:T(8,128)} %param.20) | copy-start | bytes 12582916
  5.3 6.2 %copy-start.17 = (s32[4]{0:T(128)S(1)}, s32[4]{0:T(128)}, u32[]{:S(2)}) copy-start(s32[4]{0:T(128)} %param.23) | copy-start | bytes 52
  5.3 7.4 %copy-start.16 = (f32[128]{0:T(128)S(1)}, f32[128]{0:T(128)}, u32[]{:S(2)}) copy-start(f32[128]{0:T(128)} %constant.72.clone) | copy-start | bytes 1540
  5.3 8.1 %copy-start.9 = (f32[384]{0:T(512)S(1)}, f32[384]{0:T(512)}, u32[]{:S(2)}) copy-start(f32[384]{0:T(512)} %constant.73.clone) | copy-start | bytes 4612
  5.3 8.7 %copy-start.14 = (f32[32]{0:T(128)S(1)}, f32[32]{0:T(128)}, u32[]{:S(2)}) copy-start(f32[32]{0:T(128)} %constant.95) | copy-start | bytes 388
  5.4 8.7 %copy-start.15 = (f32[32]{0:T(128)S(1)}, f32[32]{0:T(128)}, u32[]{:S(2)}) copy-start(f32[32]{0:T(128)} %constant.71.clone) | copy-start | bytes 388
  5.4 9.3 %copy-start.4 = (f32[128,128,1]{1,0,2:T(8,128)S(1)}, f32[128,128,1]{1,0,2:T(8,128)}, u32[]{:S(2)}) copy-start(f32[128,128,1]{1,0,2:T(8,128)} %constant.102) | copy-start | bytes 196612
  14.7 6.4 %copy-start.18 = (f32[256,384]{0,1:T(8,128)S(1)}, f32[256,384]{0,1:T(8,128)}, u32[]{:S(2)}) copy-start(f32[256,384]{0,1:T(8,128)} %constant.89) | copy-start | bytes 1179652
  14.7 6.4 %copy-start.19 = (f32[256,384]{0,1:T(8,128)S(1)}, f32[256,384]{0,1:T(8,128)}, u32[]{:S(2)}) copy-start(f32[256,384]{0,1:T(8,128)} %constant.74.clone) | copy-start | bytes 1179652
  14.7 6.4 %copy-start.21 = (f32[32]{0:T(128)S(1)}, f32[32]{0:T(128)}, u32[]{:S(2)}) copy-start(f32[32]{0:T(128)} %constant.91) | copy-start | bytes 388
  21.1 8.4 %copy-start.22 = (f32[384,4]{0,1:T(4,128)S(1)}, f32[384,4]{0,1:T(4,128)}, u32[]{:S(2)}) copy-start(f32[384,4]{0,1:T(4,128)} %constant.76.clone) | copy-start | bytes 18436
  21.1 8.4 %copy-start.23 = (f32[384,4]{0,1:T(4,128)S(1)}, f32[384,4]{0,1:T(4,128)}, u32[]{:S(2)}) copy-start(f32[384,4]{0,1:T(4,128)} %constant.75.clone) | copy-start | bytes 18436
  29.5 16.4 %copy-start.12 = (s32[4,2]{0,1:T(2,128)S(1)}, s32[4,2]{0,1:T(2,128)}, u32[]{:S(2)}) copy-start(s32[4,2]{0,1:T(2,128)} %param.22) | copy-start | bytes 100
  29.5 17.0 %copy-start.3 = (f32[256,256]{1,0:T(8,128)S(1)}, f32[256,256]{1,0:T(8,128)}, u32[]{:S(2)}) copy-start(f32[256,256]{1,0:T(8,128)} %constant.66.clone) | copy-start | bytes 786436
  29.6 17.6 %copy-start.13 = (f32[256]{0:T(256)S(1)}, f32[256]{0:T(256)}, u32[]{:S(2)}) copy-start(f32[256]{0:T(256)} %constant.70.clone) | copy-start | bytes 3076
  37.6 20.3 %all-to-all-start = ((f32[8,16,896]{2,1,0:T(8,128)}), f32[8,16,896]{2,1,0:T(8,128)S(1)}, u32[]{:S(2)}, u32[]{:S(2)}) async-start(f32[8,16,896]{2,1,0:T(8,128)} %pad_maximum_fusion), calls=%async_computation | async-start | bytes 917504 | tf_op jit(solution)/shard_map/all_to_all | solution.py:187
  49.1 9.2 %copy-start.2 = (f32[8,32,256,1]{2,1,0,3:T(8,128)S(1)}, f32[8,32,256,1]{2,1,0,3:T(8,128)}, u32[]{:S(2)}) copy-start(f32[8,32,256,1]{2,1,0,3:T(8,128)} %constant.103) | copy-start | bytes 786436
  49.1 9.6 %copy-start.7 = (f32[8,256]{1,0:T(8,128)S(1)}, f32[8,256]{1,0:T(8,128)}, u32[]{:S(2)}) copy-start(f32[8,256]{1,0:T(8,128)} %constant.93) | copy-start | bytes 24580
  61.9 3.9 %copy-start.1 = (f32[16,256,384]{2,1,0:T(8,128)}, f32[16,256,384]{2,1,0:T(8,128)S(1)}, u32[]{:S(2)}) copy-start(f32[16,256,384]{2,1,0:T(8,128)S(1)} %multiply_bitcast_fusion) | copy-start | bytes 18874372
  61.9 21.0 %copy-start.10 = (f32[256]{0:T(256)S(1)}, f32[256]{0:T(256)}, u32[]{:S(2)}) copy-start(f32[256]{0:T(256)} %constant.100) | copy-start | bytes 3076
  61.9 21.0 %copy-start.11 = (f32[256]{0:T(256)S(1)}, f32[256]{0:T(256)}, u32[]{:S(2)}) copy-start(f32[256]{0:T(256)} %constant.98) | copy-start | bytes 3076
  62.0 21.0 %copy-start.20 = (f32[8,2,256,1]{2,0,3,1:T(8,128)S(1)}, f32[8,2,256,1]{2,0,3,1:T(8,128)}, u32[]{:S(2)}) copy-start(f32[8,2,256,1]{2,0,3,1:T(8,128)} %constant.104) | copy-start | bytes 49156
  89.6 14.5 %all-to-all-start.1 = ((f32[8,16,578]{2,1,0:T(8,128)}), f32[8,16,578]{2,1,0:T(8,128)S(1)}, u32[]{:S(2)}, u32[]{:S(2)}) async-start(f32[8,16,578]{2,1,0:T(8,128)} %maximum_maximum_fusion), calls=%async_computation.1 | async-start | bytes 655360 | tf_op jit(solution)/shard_map/all_to_all | solution.py:249
  109.8 4.3 %copy-start.6 = (f32[256,256]{1,0:T(8,128)S(1)}, f32[256,256]{1,0:T(8,128)}, u32[]{:S(2)}) copy-start(f32[256,256]{1,0:T(8,128)} %constant.88) | copy-start | bytes 786436
